TPU v7x, 32 devices: a whole 2x2x4 slice. The times are simulated.
32 devices in a mesh: stream: 8 (over z, x), cross: 4 (over y, core).
Axes of the slice: x: 2, y: 2, z: 4, core: 2. Of those that a mesh axis runs over, the one named last changes fastest.
Arguments:
- rhs: float32 [128, 320, 128], P(('stream', 'cross')), may hold values from -240 to 240
- damping: float32 [128, 320], P(('stream', 'cross')), may hold values from 3 to 6
- omega: float32 [1], replicated, may hold values from 1 to 3
- jac_diag: bfloat16 [128, 320, 320], P(('stream', 'cross')), may hold values from -0.15625 to 0.15625
- jac_face: bfloat16 [128, 320, 480], P(('stream', 'cross')), may hold values from -0.125 to 0.125
- face_list: int32 [128, 6], P(('stream', 'cross')), may hold values from 0 to 36, as said below
- stream_sends: int32 [32, 2, 4], P(('stream', 'cross')), may hold values from 0 to 19, as said below
- cross_sends: int32 [32, 2, 2], P(('stream', 'cross')), may hold values from 0 to 23, as said below
Outputs:
- solution: float32 [128, 320, 128], P(('stream', 'cross'))
- residual: float32 [128, 320, 128], P(('stream', 'cross'))
Inputs may be any that keep to these rules, and one draw needn't show every extreme that they name: `face_list`: within each partition, each face of an element points to the opposite face of its neighbour: to a slot 6 e + f of an own element, to a received trace in the layout of the table, or to the zero last slot on radial boundaries. Every received slot is read by exactly one face. `stream_sends`: each row lists distinct own trace slots 6 e + f of streamwise faces, in the order in which the neighbour's table receives them. `cross_sends`: each row lists distinct own trace slots 6 e + f of azimuthal faces, in the order in which the neighbour's table receives them; the cross partitions close into a loop.
All inputs are finite; a program needn't handle non-finite values.
Results may differ from a plain program's by a relative error of at most 0.003.
The roundings to bfloat16 on the way count: a program that leaves them out, or rounds other values in their place, can miss the bound.
Values may be sent and summed in bfloat16 or wider, within the bound.
No kernel may reach another device: no remote copies, remote signals or barrier semaphores. Data moves between devices by JAX's collectives and lax.ppermute only.
A program may use at most 128 MiB of HBM per device.

v0:
```python
import functools
import jax
import jax.numpy as jnp
import numpy as np
from jax import lax
from jax.experimental import pallas as pl
from jax.experimental.pallas import tpu as pltpu
from jax.sharding import PartitionSpec as P

NP = 4
NVAR = 5
ITERS = 3
FACES = 6
AXES = ("stream", "cross")
HIGH = lax.Precision.HIGHEST
F32 = jnp.float32
BF16 = jnp.bfloat16
LANES = 128
NEAR = 4
VMEM_LIMIT = 20 * 2**20


def passed_along(value, axis, steps):
    count = lax.axis_size(axis)
    first, last = (max(0, -steps), min(count, count - steps))
    return lax.ppermute(value, axis, [(source, source + steps) for source in range(first, last)])


def shifted(block, axis, distance):
    devices = range(lax.axis_size(axis))
    route = [((i - distance) % len(devices), i) for i in devices]
    return lax.ppermute(block, axis, route)


def total(block):
    count = lax.axis_size(AXES[0]) * lax.axis_size(AXES[1])
    rows, width = block.shape
    share = -(-rows // count)
    if share * count != rows:
        block = jnp.pad(block, ((0, share * count - rows), (0, 0)))
    parts = lax.all_to_all(block.reshape(count, share, width), AXES, 0, 0)
    (mine,) = call(add_up_kernel, "add_up", [parts], [(parts.shape, F32)], limit=4 * 2**20)
    return lax.all_to_all(mine, AXES, 0, 0).reshape(count * share, width)[:rows]


def mm(left, right):
    return jnp.dot(left, right, precision=HIGH, preferred_element_type=F32)


def mm_tn(left, right):
    return lax.dot_general(
        left, right, (((0,), (0,)), ((), ())), precision=HIGH, preferred_element_type=F32
    )


def mm_nt(left, right):
    return lax.dot_general(
        left, right, (((1,), (1,)), ((), ())), precision=HIGH, preferred_element_type=F32
    )


def grid_of(shape, axis):
    return lax.broadcasted_iota(jnp.int32, shape, axis)


def identity(size):
    return jnp.where(grid_of((size, size), 0) == grid_of((size, size), 1), 1.0, 0.0).astype(F32)


def pivot_block(corner):
    size = corner.shape[0]
    columns = [jnp.broadcast_to(corner[:, t : t + 1], (size, LANES)) for t in range(size)]
    left = [[jnp.broadcast_to(columns[j][i : i + 1], (size, LANES)) for j in range(i + 1)] for i in range(size)]
    lower = [[None] * size for _ in range(size)]
    scales = []
    for j in range(size):
        scales.append(lax.rsqrt(left[j][j]))
        for i in range(j + 1, size):
            lower[i][j] = left[i][j] * scales[j]
        for i in range(j + 1, size):
            for k in range(j + 1, i + 1):
                left[i][k] = left[i][k] - lower[i][j] * lower[k][j]
    return lower, scales


def factor(gram):
    size = gram.shape[0]
    step = 8
    unit = identity(size)
    sides = [[m[r : r + step] for r in range(0, size, step)] for m in (gram, unit)]
    row = grid_of((step, size), 0)
    for p in range(size // step):
        base = p * step
        lower, scales = pivot_block(sides[0][p][:, base : base + step])
        leads = []
        for side in sides:
            rows = [jnp.broadcast_to(side[p][t : t + 1], (step, size)) for t in range(step)]
            for t in range(step):
                rows[t] = rows[t] * scales[t]
                for u in range(t + 1, step):
                    rows[u] = rows[u] - lower[u][t] * rows[t]
            strip = rows[0]
            for t in range(1, step):
                strip = jnp.where(row == t, rows[t], strip)
            side[p] = strip
            leads.append(rows)
        far = min(p + 1 + NEAR, size // step)
        for q in range(p + 1, far):
            strip = sides[0][q]
            columns = [jnp.broadcast_to(strip[:, base + t : base + t + 1], (step, size)) for t in range(step)]
            for t in range(step):
                share = columns[t] * scales[t]
                for u in range(t + 1, step):
                    columns[u] = columns[u] - share * lower[u][t]
                for side, lead in zip(sides, leads):
                    side[q] = side[q] - share * lead[t]
        if far * step < size:
            done = jnp.concatenate([side[p] for side in sides], 1)
            update = mm_tn(done[:, far * step : size], done)
            for q in range(far, size // step):
                at = (q - far) * step
                for k, side in enumerate(sides):
                    side[q] = side[q] - update[at : at + step, k * size : (k + 1) * size]
    upper = jnp.concatenate(sides[0], 0)
    upper = jnp.where(grid_of((size, size), 1) >= grid_of((size, size), 0), upper, 0.0)
    return upper, jnp.concatenate(sides[1], 0)


def rows_of(element, rows):
    return pl.ds(pl.multiple_of(element * rows, rows), rows)


def lanes_of(half, width):
    return pl.ds(pl.multiple_of(half * width, width), width)


def split(value):
    high = value.astype(BF16)
    return high, (value - high.astype(F32)).astype(BF16)


def take_traces(element, rows, picks_ref, field_ref, traces_ref):
    size = traces_ref.shape[1]
    rounded = field_ref[rows_of(element, rows), :].astype(BF16)
    picked = jnp.dot(picks_ref[...], rounded, preferred_element_type=F32).astype(BF16)
    for face in range(FACES):
        traces_ref[element * FACES + face] = picked[face * size : (face + 1) * size, :]


def pack(sends_ref, traces_ref, out_refs):
    for row, out_ref in enumerate(out_refs):
        for item in range(out_ref.shape[0]):
            out_ref[item] = traces_ref[sends_ref[0, row, item]]


def add_up_kernel(parts_ref, out_ref):
    out_ref[...] = jnp.broadcast_to(jnp.sum(parts_ref[...], axis=0, keepdims=True), out_ref.shape)


def start_gram_kernel(rhs_ref, damping_ref, out_ref):
    field = rhs_ref[...]
    width = field.shape[-1]
    gram = mm_tn(field, field)
    mass = jnp.sum(jnp.sum(damping_ref[...], axis=1, keepdims=True), axis=0, keepdims=True)
    corner = (grid_of(gram.shape, 0) == width - 1) & (grid_of(gram.shape, 1) == 0)
    out_ref[...] = jnp.where(corner, mass, gram)


def start_kernel(
    cells, gram_ref, rhs_ref, picks_ref, ssend_ref, csend_ref,
    field_ref, traces_ref, s0_ref, s1_ref, c0_ref, c1_ref, upper_ref, inverse_ref, center_ref,
):
    width = rhs_ref.shape[-1]
    half = width // 2
    count = traces_ref.shape[0] // FACES
    rows = rhs_ref.shape[0] // count
    raw = gram_ref[...]
    r, c = grid_of(raw.shape, 0), grid_of(raw.shape, 1)
    corner = (r == width - 1) & (c == 0)
    mass = raw[width - 1 : width, 0:1]
    raw = jnp.where(corner, raw[0:1, width - 1 : width], raw)
    center_ref[...] = jnp.broadcast_to(mass * (1.0 / cells), center_ref.shape)
    rr, ri = raw[:half, :half], raw[:half, half:]
    ir, ii = raw[half:, :half], raw[half:, half:]
    same, other = rr + ii, ir - ri
    gram = jnp.concatenate(
        [jnp.concatenate([same, other], 1), jnp.concatenate([-other, same], 1)], 0
    )
    upper, inverse = factor(gram)
    upper_ref[...] = upper
    inverse_ref[...] = inverse
    turn = inverse.T
    first = jnp.concatenate([turn[:half], -turn[half:]], 0)
    second = jnp.concatenate([turn[half:], turn[:half]], 0)
    wide = jnp.concatenate([first, second], 1)

    @pl.loop(0, count)
    def _(e):
        field_ref[rows_of(e, rows), :] = mm(rhs_ref[rows_of(e, rows), :], wide)
        take_traces(e, rows, picks_ref, field_ref, traces_ref)

    pack(ssend_ref, traces_ref, (s0_ref, s1_ref))
    pack(csend_ref, traces_ref, (c0_ref, c1_ref))


def next_kernel(
    level, red_ref, image_ref, *refs,
):
    basis = refs[: level + 1]
    picks_ref, ssend_ref, csend_ref = refs[level + 1 : level + 4]
    field_ref, traces_ref, s0_ref, s1_ref, c0_ref, c1_ref, upper_ref, inverse_ref = refs[level + 4 :]
    width = red_ref.shape[-1]
    blocks = [red_ref[j * width : (j + 1) * width, :] for j in range(level + 2)]
    coeffs = jnp.concatenate(blocks[:-1], 1)
    gram = blocks[-1] - mm_nt(coeffs, coeffs)
    upper, inverse = factor(gram)
    upper_ref[...] = upper
    inverse_ref[...] = inverse
    turn = inverse.T
    matrix = jnp.concatenate([turn, -mm_tn(coeffs, turn)], 0)
    count = traces_ref.shape[0] // FACES
    rows = field_ref.shape[0] // count

    @pl.loop(0, count)
    def _(e):
        at = rows_of(e, rows)
        for h in range(2):
            cut = slice(h * width, (h + 1) * width)
            parts = [ref[at, cut] for ref in (image_ref,) + basis]
            field_ref[at, cut] = mm(jnp.concatenate(parts, 1), matrix)
        take_traces(e, rows, picks_ref, field_ref, traces_ref)

    pack(ssend_ref, traces_ref, (s0_ref, s1_ref))
    pack(csend_ref, traces_ref, (c0_ref, c1_ref))


def turned(matrix):
    half = matrix.shape[0] // 2
    return jnp.concatenate([-matrix[half:], matrix[:half]], 0)


def inner_kernel(
    omega_ref, center_ref, damping_ref, diag_ref, field_ref, upper_ref, inverse_ref, *refs,
):
    part_ref, shift_ref, chain_out, unchain_out = refs[-4:]
    chain_refs = refs[:-4]
    chain, unchain = upper_ref[...], inverse_ref[...].T
    if chain_refs:
        chain = mm(chain, chain_refs[0][...])
        unchain = mm(chain_refs[1][...], unchain)
    chain_out[...] = chain
    unchain_out[...] = unchain
    omega = omega_ref[0]
    center = center_ref[0:1, 0:1]
    twist = omega * mm(chain, turned(unchain))
    shift_ref[...] = (twist + center * identity(twist.shape[0])).T
    width = twist.shape[0]
    rows = diag_ref.shape[1]

    @pl.loop(0, diag_ref.shape[0])
    def _(e):
        at = rows_of(e, rows)
        re, im = field_ref[at, :width], field_ref[at, width:]
        local = jnp.dot(diag_ref[e], field_ref[at, :].astype(BF16), preferred_element_type=F32)
        scale = jnp.swapaxes(damping_ref[pl.ds(e, 1), :] - center, 0, 1)
        part_ref[at, :width] = local[:, :width] + scale * re - omega * im - mm(re, twist)
        part_ref[at, width:] = local[:, width:] + scale * im + omega * re - mm(im, twist)


def square_kernel(
    sums0_ref, sums1_ref, shift0_ref, shift1_ref, shift2_ref, s0_ref, i1_ref, i2_ref, pack_ref,
):
    width = s0_ref.shape[0]
    t00 = sums0_ref[:width, :] + shift0_ref[...]
    t01 = sums1_ref[:width, :]
    t11 = sums1_ref[width : 2 * width, :] + shift1_ref[...]
    n1 = -mm(i1_ref[...], t00)
    n2 = -mm(i2_ref[...], t01 + mm(t11, n1))
    gram = identity(width) + mm_tn(n1, n1) + mm_tn(n2, n2)
    _, inverse = factor(gram)
    turn = inverse.T
    items = (turn, mm(n1, turn), mm(n2, turn), mm(inverse, s0_ref[...]), i1_ref[...], i2_ref[...])
    for at, item in enumerate(items + (mm_tn(i1_ref[...], t11.T), shift2_ref[...])):
        pack_ref[at] = item


def outer_kernel(level, list_ref, traces_ref, prev_ref, next_ref, cprev_ref, cnext_ref,
                 face_ref, part_ref, *refs):
    basis = refs[: level + 1]
    image_ref, out_ref, table, nearby = refs[level + 1 :]
    own = traces_ref.shape[0]
    size = traces_ref.shape[1]
    at = 0
    for ref in (traces_ref, prev_ref, next_ref, cprev_ref, cnext_ref):
        table[at : at + ref.shape[0]] = ref[...]
        at += ref.shape[0]
    table[at] = jnp.zeros(table.shape[1:], table.dtype)
    count, rows = face_ref.shape[:2]
    width = part_ref.shape[-1] // 2

    @pl.loop(0, count)
    def _(e):
        for f in range(FACES):
            nearby[f * size : (f + 1) * size, :] = table[list_ref[e, f]]
        coupled = jnp.dot(face_ref[e], nearby[...], preferred_element_type=F32)
        image_ref[rows_of(e, rows), :] = part_ref[rows_of(e, rows), :] + coupled

    out_ref[...] = jnp.zeros_like(out_ref)
    piece = 2 * width if (count * rows) % (2 * width) == 0 else rows

    @pl.loop(0, count * rows // piece)
    def _(i):
        @pl.loop(0, 2)
        def _(h):
            at = (rows_of(i, piece), lanes_of(h, width))
            parts = [split(ref[at]) for ref in basis + (image_ref,)]
            left = jnp.concatenate(parts[-1], 1)
            right = jnp.concatenate([jnp.concatenate([p[k] for p in parts], 1) for k in range(2)], 0)
            term = lax.dot_general(
                jnp.concatenate([left, left], 0),
                right,
                (((0,), (0,)), ((), ())),
                preferred_element_type=F32,
            )
            term = term[:width] + term[width:]
            for j in range(level + 2):
                out_ref[j * width : (j + 1) * width, :] += term[:, j * width : (j + 1) * width]


def final_kernel(
    red_ref, image_ref, v0_ref, v1_ref, v2_ref, pack_ref, solution_ref, residual_ref,
    fields, small, solved, left_over, in_sems, out_sems,
):
    load = pltpu.make_async_copy(pack_ref, small, in_sems.at[4])
    load.start()
    loads = [
        pltpu.make_async_copy(ref, fields.at[j], in_sems.at[j])
        for j, ref in enumerate((v0_ref, v1_ref, v2_ref, image_ref))
    ]
    for copy in loads:
        copy.start()
    width = red_ref.shape[-1]
    half = width // 2
    blocks = [red_ref[j * width : (j + 1) * width, :] for j in range(4)]
    coeffs = jnp.concatenate(blocks[:-1], 1)
    gram = blocks[-1] - mm_nt(coeffs, coeffs)
    load.wait()
    reach_in = small[0:3].reshape(3 * width, width)
    right, i1, i2, mixed, shift2 = [small[k] for k in range(3, 8)]
    shifted_coeffs = jnp.concatenate([coeffs[:, : 2 * width], coeffs[:, 2 * width :] + shift2], 1)
    reach = mm(shifted_coeffs, reach_in)
    goal = mm(reach, right)
    _, iq = factor(gram + mm_nt(reach, reach))
    y2 = mm_tn(iq, mm(iq, goal))
    z = mm(reach_in, right - mm_tn(reach, y2))
    z = [z[k * width : (k + 1) * width] for k in range(3)]
    hy = mm_tn(jnp.concatenate([coeffs, shift2], 1), y2)
    hy = [hy[k * width : (k + 1) * width] for k in range(4)]
    y1 = -mm_tn(i2, z[2] + hy[2] + hy[3])
    y0 = -mm_tn(i1, z[1] + hy[1]) - mm(mixed, y1)
    left = grid_of((width, width), 1) < half
    rows = []
    for y, w in ((y0, z[0] + hy[0]), (y1, z[1] + hy[1]), (y2, z[2] + hy[2]), (0.0 * y2, -y2)):
        rows.append(jnp.where(left, y, pltpu.roll(w, half, 1)))
    matrix = jnp.concatenate(rows, 0)
    count = out_sems.shape[1]
    size = solved.shape[0] // count
    lanes = grid_of((size, width), 1) < half
    for copy in loads:
        copy.wait()

    def copies(e):
        at = rows_of(e, size)
        return [
            pltpu.make_async_copy(solved.at[at], solution_ref.at[at], out_sems.at[0, e]),
            pltpu.make_async_copy(left_over.at[at], residual_ref.at[at], out_sems.at[1, e]),
        ]

    @pl.loop(0, count)
    def _(e):
        at = rows_of(e, size)

        cuts = [slice(h * width, (h + 1) * width) for h in range(2)]
        first, second = [
            mm(jnp.concatenate([fields[j, at, cut] for j in range(4)], 1), matrix) for cut in cuts
        ]
        solved[at, :] = jnp.where(lanes, first, pltpu.roll(second, half, 1))
        left_over[at, :] = jnp.where(lanes, pltpu.roll(first, half, 1), second)
        for copy in copies(e):
            copy.start()

    for e in range(count):
        for copy in copies(e):
            copy.wait()


def face_rows():
    grid = np.arange(NVAR * NP * NP * NP).reshape(NVAR, NP, NP, NP)
    faces = [
        grid[:, 0],
        grid[:, NP - 1],
        grid[:, :, 0],
        grid[:, :, NP - 1],
        grid[:, :, :, 0],
        grid[:, :, :, NP - 1],
    ]
    return np.concatenate([item.reshape(-1) for item in faces]).astype(np.int32)


VM = pl.BlockSpec(memory_space=pltpu.VMEM)
SM = pl.BlockSpec(memory_space=pltpu.SMEM)
AN = pl.BlockSpec(memory_space=pl.ANY)


def call(
    kernel, name, args, outs, scratch=(), scalars=(), flops=0, limit=VMEM_LIMIT, apart=(), out_apart=()
):
    moved = sum(a.size * a.dtype.itemsize for a in args)
    return pl.pallas_call(
        kernel,
        name=name,
        out_shape=[jax.ShapeDtypeStruct(shape, dtype) for shape, dtype in outs],
        in_specs=[SM if i in scalars else AN if i in apart else VM for i in range(len(args))],
        out_specs=[AN if i in out_apart else VM for i in range(len(outs))],
        scratch_shapes=list(scratch),
        compiler_params=pltpu.CompilerParams(vmem_limit_bytes=limit),
        cost_estimate=pl.CostEstimate(flops=flops, bytes_accessed=moved, transcendentals=0),
    )(*args)


def body(rhs, damping, omega, jac_diag, jac_face, face_list, stream_sends, cross_sends):
    count, rows, blocksize = rhs.shape
    columns = 2 * blocksize
    size = NVAR * NP * NP
    slots = count * FACES
    ss, sc = stream_sends.shape[-1], cross_sends.shape[-1]
    devices = lax.axis_size("stream") * lax.axis_size("cross")
    picks = np.zeros((FACES * size, rows), np.float32)
    picks[np.arange(FACES * size), face_rows()] = 1.0
    picks = jnp.asarray(picks, BF16)
    square = ((blocksize, blocksize), F32)
    field_out = ((count * rows, columns), F32)
    rhs = rhs.reshape(count * rows, blocksize)
    stage = [
        field_out,
        ((slots, size, columns), BF16),
        ((ss, size, columns), BF16),
        ((ss, size, columns), BF16),
        ((sc, size, columns), BF16),
        ((sc, size, columns), BF16),
        square,
        square,
    ]

    (gram,) = call(start_gram_kernel, "start_gram", [rhs, damping], [square])
    gram = total(gram)
    cells = float(devices * count * rows)
    field, traces, s0, s1, c0, c1, upper, inverse, center = call(
        functools.partial(start_kernel, cells),
        "start",
        [gram, rhs, picks, stream_sends, cross_sends],
        stage + [((8, blocksize), F32)],
        [],
        (3, 4),
    )
    basis, uppers, inverses, shifts, reduced = [field], [upper], [inverse], [], []
    chains = []
    for step in range(ITERS):
        from_prev = passed_along(s0, "stream", 1)
        from_next = passed_along(s1, "stream", -1)
        cross_prev = shifted(c0, "cross", 1)
        cross_next = shifted(c1, "cross", -1)
        part, shift, *chains = call(
            inner_kernel,
            "inner",
            [omega, center, damping, jac_diag, field, upper, inverse] + chains,
            [field_out, square, square, square],
            (),
            (0,),
            10**9,
        )
        shifts.append(shift)
        if step == ITERS - 1:
            (known,) = call(
                square_kernel,
                "square",
                reduced + shifts + [uppers[0], inverses[1], inverses[2]],
                [((8, blocksize, blocksize), F32)],
                (),
                (),
                10**9,
            )
        blocks = 2 if step == 0 else 4
        image, sums = call(
            functools.partial(outer_kernel, step),
            "outer",
            [face_list, traces, from_prev, from_next, cross_prev, cross_next, jac_face, part]
            + basis,
            [field_out, ((blocks * blocksize, blocksize), F32)],
            [
                pltpu.VMEM((slots + 2 * ss + 2 * sc + 1, size, columns), BF16),
                pltpu.VMEM((FACES * size, columns), BF16),
            ],
            (0,),
        )
        sums = total(sums)
        if step < ITERS - 1:
            reduced.append(sums)
            field, traces, s0, s1, c0, c1, upper, inverse = call(
                functools.partial(next_kernel, step),
                "next",
                [sums, image] + basis + [picks, stream_sends, cross_sends],
                stage,
                [],
                (step + 4, step + 5),
            )
            basis.append(field)
            uppers.append(upper)
            inverses.append(inverse)
    out = ((count * rows, blocksize), F32)
    results = call(
        final_kernel,
        "final",
        [sums, image] + basis + [known],
        [out, out],
        [
            pltpu.VMEM((4,) + field_out[0], F32),
            pltpu.VMEM((8, blocksize, blocksize), F32),
            pltpu.VMEM(*out),
            pltpu.VMEM(*out),
            pltpu.SemaphoreType.DMA((5,)),
            pltpu.SemaphoreType.DMA((2, count)),
        ],
        (),
        0,
        None,
        range(1, 6),
        (0, 1),
    )
    return tuple(item.reshape(count, rows, blocksize) for item in results)


def solution(mesh):
    in_specs = (
        P(("stream", "cross"), None, None),
        P(("stream", "cross"), None),
        P(),
        P(("stream", "cross"), None, None),
        P(("stream", "cross"), None, None),
        P(("stream", "cross"), None),
        P(("stream", "cross"), None, None),
        P(("stream", "cross"), None, None),
    )
    out_specs = (P(("stream", "cross"), None, None), P(("stream", "cross"), None, None))
    return jax.shard_map(body, mesh=mesh, in_specs=in_specs, out_specs=out_specs, check_vma=False)
```

profile of v0, /device:TPU:0, one launch (start us, length us, event | category | flops | bytes accessed | tf_op | source)
XLA Modules:
  0.0 194.1 jit_solution(9262211292861185495)
XLA Ops:
  3.2 14.5 %all_to_all.40.parts_ref = f32[32,4,128]{2,1,0:T(4,128)S(1)} all-to-all(f32[32,4,128]{2,1,0:T(4,128)S(1)} %bitcast.20), channel_id=1, replica_groups=mesh['stream'=8,'cross'=4] {'stream','cross'}, dimensions={0} | all-to-all | bytes 131072 | tf_op jit(solution)/shard_map/all_to_all | solution.py:41
  17.8 9.1 %all_to_all.41 = f32[32,4,128]{2,1,0:T(4,128)S(1)} all-to-all(f32[32,4,128]{2,1,0:T(4,128)S(1)} %add_up.4), channel_id=1, replica_groups=mesh['stream'=8,'cross'=4] {'stream','cross'}, dimensions={0} | all-to-all | bytes 131072 | tf_op jit(solution)/shard_map/all_to_all | solution.py:43
  28.3 8.4 %start.1 = (f32[1280,256]{1,0:T(8,128)S(1)}, bf16[24,80,256]{2,1,0:T(8,128)(2,1)S(1)}, bf16[4,80,256]{2,1,0:T(8,128)(2,1)S(1)}, bf16[4,80,256]{2,1,0:T(8,128)(2,...) custom-call(f32[128,128]{1,0:T(8,128)S(1)} %bitcast.17, ...), custom_call_target="tpu_custom_call" | custom-call | bytes 1028144 | tf_op jit(solution)/shard_map/start/pallas_call | solution.py:419
  36.7 2.5 %collective-permute-start = (bf16[4,80,256]{2,1,0:T(8,128)(2,1)S(1)}, bf16[4,80,256]{2,1,0:T(8,128)(2,1)S(1)}, u32[]{:S(2)}, u32[]{:S(2)}) collective-permute-start(bf16[4,80,256]{2,1,0:T(8,128)(2,1)S(1)} %get-tuple-element.46), channel_id=1, source_target_pairs={{0,4},{4,8},{8,12},{12,16},{16,20},{20,24},{24,28},{1,5},{5,9},{9,... | collective-permute-start | bytes 491528 | tf_op jit(solution)/shard_map/ppermute | solution.py:26
  44.2 2.5 %inner.3 = (f32[1280,256]{1,0:T(8,128)S(1)}, f32[128,128]{1,0:T(8,128)S(1)}, f32[128,128]{1,0:T(8,128)S(1)}, f32[128,128]{1,0:T(8,128)S(1)}) custom-call(f32[1]{0:T(128)S(6)} %copy.11.omega_ref, f32[8,128]{1,0:T(8,128)S(1)} %get-tuple-element.50.center_ref, f32[4,320]{1,0:T(4,128)S(1)} %copy-done.14, bf16[4,320,320]{2,1,0:T(8,128)(2,1)S(1)} %copy-done.15, ...), custom_call_target="tpu_custom_call" | custom-call | flops 1000000000 | bytes 2270212 | tf_op jit(solution)/shard_map/inner/pallas_call | solution.py:419
  47.0 4.2 %outer.3 = (f32[1280,256]{1,0:T(8,128)S(1)}, f32[256,128]{1,0:T(8,128)S(1)}) custom-call(s32[4,6]{1,0:T(4,128)S(1)} %copy-done.8, bf16[24,80,256]{2,1,0:T(8,128)(2,1)S(1)} %get-tuple-element.45.traces_ref, bf16[4,80,256]{2,1,0:T(8,128)(2,1)S(1)} %collective-permute-done.prev_ref, bf16[4,80,256]{2,1,0:T(8,128)(2,1)S(1)} %collective-permute-done.1.next_ref, ...), custom_call_target="tpu_custom_call" | custom-call | bytes 5324896 | tf_op jit(solution)/shard_map/outer/pallas_call | solution.py:419
  51.2 11.9 %all_to_all.42.parts_ref = f32[32,8,128]{2,1,0:T(8,128)S(1)} all-to-all(f32[32,8,128]{2,1,0:T(8,128)S(1)} %bitcast.21), channel_id=1, replica_groups=mesh['stream'=8,'cross'=4] {'stream','cross'}, dimensions={0} | all-to-all | bytes 262144 | tf_op jit(solution)/shard_map/all_to_all | solution.py:41
  63.2 10.0 %all_to_all.43 = f32[32,8,128]{2,1,0:T(8,128)S(1)} all-to-all(f32[32,8,128]{2,1,0:T(8,128)S(1)} %add_up.5), channel_id=1, replica_groups=mesh['stream'=8,'cross'=4] {'stream','cross'}, dimensions={0} | all-to-all | bytes 262144 | tf_op jit(solution)/shard_map/all_to_all | solution.py:43
  73.1 8.8 %next.2 = (f32[1280,256]{1,0:T(8,128)S(1)}, bf16[24,80,256]{2,1,0:T(8,128)(2,1)S(1)}, bf16[4,80,256]{2,1,0:T(8,128)(2,1)S(1)}, bf16[4,80,256]{2,1,0:T(8,128)(2,1...) custom-call(f32[256,128]{1,0:T(8,128)S(1)} %bitcast.15, ...), custom_call_target="tpu_custom_call" | custom-call | bytes 3059760 | tf_op jit(solution)/shard_map/next/pallas_call | solution.py:419
  82.0 2.6 %collective-permute-start.4 = (bf16[4,80,256]{2,1,0:T(8,128)(2,1)S(1)}, bf16[4,80,256]{2,1,0:T(8,128)(2,1)S(1)}, u32[]{:S(2)}, u32[]{:S(2)}) collective-permute-start(bf16[4,80,256]{2,1,0:T(8,128)(2,1)S(1)} %get-tuple-element.58), channel_id=1, source_target_pairs={{0,4},{4,8},{8,12},{12,16},{16,20},{20,24},{24,28},{1,5},{5,9},{9,... | collective-permute-start | bytes 491528 | tf_op jit(solution)/shard_map/ppermute | solution.py:26
  85.9 1.7 collective-permute-start.7
  87.7 2.8 %inner.4 = (f32[1280,256]{1,0:T(8,128)S(1)}, f32[128,128]{1,0:T(8,128)S(1)}, f32[128,128]{1,0:T(8,128)S(1)}, f32[128,128]{1,0:T(8,128)S(1)}) custom-call(f32[1]{0:T(128)S(6)} %copy.11.omega_ref, f32[8,128]{1,0:T(8,128)S(1)} %get-tuple-element.50.center_ref, f32[4,320]{1,0:T(4,128)S(1)} %copy-done.14, bf16[4,320,320]{2,1,0:T(8,128)(2,1)S(1)} %copy-done.16, ...), custom_call_target="tpu_custom_call" | custom-call | flops 1000000000 | bytes 2401284 | tf_op jit(solution)/shard_map/inner/pallas_call | solution.py:419
  92.2 5.0 %outer.4 = (f32[1280,256]{1,0:T(8,128)S(1)}, f32[512,128]{1,0:T(8,128)S(1)}) custom-call(s32[4,6]{1,0:T(4,128)S(1)} %copy-done.8, bf16[24,80,256]{2,1,0:T(8,128)(2,1)S(1)} %get-tuple-element.57.traces_ref, bf16[4,80,256]{2,1,0:T(8,128)(2,1)S(1)} %collective-permute-done.4.prev_ref, bf16[4,80,256]{2,1,0:T(8,128)(2,1)S(1)} %collective-permute-done.5.next_ref, ...), custom_call_target="tpu_custom_call" | custom-call | bytes 6635616 | tf_op jit(solution)/shard_map/outer/pallas_call | solution.py:419
  97.2 14.2 %all_to_all.44.parts_ref = f32[32,16,128]{2,1,0:T(8,128)S(1)} all-to-all(f32[32,16,128]{2,1,0:T(8,128)S(1)} %bitcast.18), channel_id=1, replica_groups=mesh['stream'=8,'cross'=4] {'stream','cross'}, dimensions={0} | all-to-all | bytes 524288 | tf_op jit(solution)/shard_map/all_to_all | solution.py:41
  111.5 12.8 %all_to_all.45 = f32[32,16,128]{2,1,0:T(8,128)S(1)} all-to-all(f32[32,16,128]{2,1,0:T(8,128)S(1)} %add_up.6), channel_id=1, replica_groups=mesh['stream'=8,'cross'=4] {'stream','cross'}, dimensions={0} | all-to-all | bytes 524288 | tf_op jit(solution)/shard_map/all_to_all | solution.py:43
  124.3 9.8 %next.3 = (f32[1280,256]{1,0:T(8,128)S(1)}, bf16[24,80,256]{2,1,0:T(8,128)(2,1)S(1)}, bf16[4,80,256]{2,1,0:T(8,128)(2,1)S(1)}, bf16[4,80,256]{2,1,0:T(8,128)(2,1...) custom-call(f32[512,128]{1,0:T(8,128)S(1)} %bitcast.13, ...), custom_call_target="tpu_custom_call" | custom-call | bytes 4501552 | tf_op jit(solution)/shard_map/next/pallas_call | solution.py:419
  134.1 2.8 %collective-permute-start.8 = (bf16[4,80,256]{2,1,0:T(8,128)(2,1)S(1)}, bf16[4,80,256]{2,1,0:T(8,128)(2,1)S(1)}, u32[]{:S(2)}, u32[]{:S(2)}) collective-permute-start(bf16[4,80,256]{2,1,0:T(8,128)(2,1)S(1)} %get-tuple-element.71), channel_id=1, source_target_pairs={{0,4},{4,8},{8,12},{12,16},{16,20},{20,24},{24,28},{1,5},{5,9},{9,... | collective-permute-start | bytes 491528 | tf_op jit(solution)/shard_map/ppermute | solution.py:26
  140.0 3.0 %inner.5 = (f32[1280,256]{1,0:T(8,128)S(1)}, f32[128,128]{1,0:T(8,128)S(1)}, f32[128,128]{1,0:T(8,128)}, f32[128,128]{1,0:T(8,128)}) custom-call(f32[1]{0:T(128)S(6)} %copy.11.omega_ref, f32[8,128]{1,0:T(8,128)S(1)} %get-tuple-element.50.center_ref, f32[4,320]{1,0:T(4,128)S(1)} %copy-done.14, bf16[4,320,320]{2,1,0:T(8,128)(2,1)S(1)} %copy-done.16, ...), custom_call_target="tpu_custom_call" | custom-call | flops 1000000000 | bytes 2401284 | tf_op jit(solution)/shard_map/inner/pallas_call | solution.py:419
  144.2 5.0 %outer.5 = (f32[1280,256]{1,0:T(8,128)S(1)}, f32[512,128]{1,0:T(8,128)S(1)}) custom-call(s32[4,6]{1,0:T(4,128)S(1)} %copy-done.8, bf16[24,80,256]{2,1,0:T(8,128)(2,1)S(1)} %get-tuple-element.70.traces_ref, bf16[4,80,256]{2,1,0:T(8,128)(2,1)S(1)} %collective-permute-done.8.prev_ref, bf16[4,80,256]{2,1,0:T(8,128)(2,1)S(1)} %collective-permute-done.9.next_ref, ...), custom_call_target="tpu_custom_call" | custom-call | bytes 7946336 | tf_op jit(solution)/shard_map/outer/pallas_call | solution.py:419
  150.2 14.6 %all_to_all.46.parts_ref = f32[32,16,128]{2,1,0:T(8,128)S(1)} all-to-all(f32[32,16,128]{2,1,0:T(8,128)S(1)} %bitcast.19), channel_id=1, replica_groups=mesh['stream'=8,'cross'=4] {'stream','cross'}, dimensions={0} | all-to-all | bytes 524288 | tf_op jit(solution)/shard_map/all_to_all | solution.py:41
  165.6 2.8 %all-to-all-start.7 = ((f32[32,16,128]{2,1,0:T(8,128)}), f32[32,16,128]{2,1,0:T(8,128)S(1)}, u32[]{:S(2)}, u32[]{:S(2)}) async-start(f32[32,16,128]{2,1,0:T(8,128)} %add_up.7), calls=%async_computation.7 | async-start | bytes 524288 | tf_op jit(solution)/shard_map/all_to_all | solution.py:43
  168.4 5.3 %square.1.pack_ref = f32[8,128,128]{2,1,0:T(8,128)S(1)} custom-call(f32[256,128]{1,0:T(8,128)S(1)} %bitcast.16, f32[512,128]{1,0:T(8,128)S(1)} %bitcast.14, f32[128,128]{1,0:T(8,128)S(1)} %get-tuple-element.83.shift0_ref, f32[128,128]{1,0:T(8,128)S(1)} %get-tuple-element.84.shift1_ref, f32[128,128]{1,0:T(8,128)S(1)} %get-tuple-element.85.shift2_ref, ...), custom_call_target="tpu_custom_call" | custom-call | flops 1000000000 | bytes 786432 | tf_op jit(solution)/shard_map/square/pallas_call | solution.py:419
  174.5 4.3 %all-to-all-done.7 = f32[32,16,128]{2,1,0:T(8,128)S(1)} async-done(((f32[32,16,128]{2,1,0:T(8,128)}), f32[32,16,128]{2,1,0:T(8,128)S(1)}, u32[]{:S(2)}, u32[]{:S(2)}) %all-to-all-start.7) | async-done | bytes 262176 | tf_op jit(solution)/shard_map/all_to_all | solution.py:43
  179.5 14.4 %final.1 = (f32[1280,128]{1,0:T(8,128)}, f32[1280,128]{1,0:T(8,128)}) custom-call(f32[512,128]{1,0:T(8,128)} %bitcast.22, f32[1280,256]{1,0:T(8,128)} %copy-done.6, f32[1280,256]{1,0:T(8,128)} %copy-done, f32[1280,256]{1,0:T(8,128)} %copy-done.1, f32[1280,256]{1,0:T(8,128)} %copy-done.3, f32[8,128,128]{2,1,0:T(8,128)} %copy-done.7), custom_call_target="tpu_custom_call" | custom-call | bytes 6029312 | tf_op jit(solution)/shard_map/final/pallas_call | solution.py:419
  (61 shorter events, 19.1 us)
Async XLA Ops:
  0.6 26.3 %copy-start.4 = (bf16[480,320]{1,0:T(8,128)(2,1)S(1)}, bf16[480,320]{1,0:T(8,128)(2,1)}, u32[]{:S(2)}) copy-start(bf16[480,320]{1,0:T(8,128)(2,1)} %constant.2.clone.picks_ref.refs_1_.refs_2_) | copy-start | bytes 921604
  2.5 40.5 %copy-start.14 = (f32[4,320]{1,0:T(4,128)S(1)}, f32[4,320]{1,0:T(4,128)}, u32[]{:S(2)}) copy-start(f32[4,320]{1,0:T(4,128)} %damping_ref.7) | copy-start | bytes 15364
  36.7 107.5 %copy-start = (f32[1280,256]{1,0:T(8,128)}, f32[1280,256]{1,0:T(8,128)S(1)}, u32[]{:S(2)}) copy-start(f32[1280,256]{1,0:T(8,128)S(1)} %get-tuple-element.51.field_ref.refs_0_.v0_ref) | copy-start | bytes 3932164
  36.7 10.1 %collective-permute-start = (bf16[4,80,256]{2,1,0:T(8,128)(2,1)S(1)}, bf16[4,80,256]{2,1,0:T(8,128)(2,1)S(1)}, u32[]{:S(2)}, u32[]{:S(2)}) collective-permute-start(bf16[4,80,256]{2,1,0:T(8,128)(2,1)S(1)} %get-tuple-element.46), channel_id=1, source_target_pairs={{0,4},{4,8},{8,12},{12,16},{16,20},{20,24},{24,28},{1,5},{5,9},{9,... | collective-permute-start | bytes 491528 | tf_op jit(solution)/shard_map/ppermute | solution.py:26
  39.2 7.7 %collective-permute-start.1 = (bf16[4,80,256]{2,1,0:T(8,128)(2,1)S(1)}, bf16[4,80,256]{2,1,0:T(8,128)(2,1)S(1)}, u32[]{:S(2)}, u32[]{:S(2)}) collective-permute-start(bf16[4,80,256]{2,1,0:T(8,128)(2,1)S(1)} %get-tuple-element.47), channel_id=1, source_target_pairs={{4,0},{8,4},{12,8},{16,12},{20,16},{24,20},{28,24},{5,1},{9,5},{13... | collective-permute-start | bytes 491528 | tf_op jit(solution)/shard_map/ppermute | solution.py:26
  41.2 5.6 %collective-permute-start.2 = (bf16[2,80,256]{2,1,0:T(8,128)(2,1)S(1)}, bf16[2,80,256]{2,1,0:T(8,128)(2,1)S(1)}, u32[]{:S(2)}, u32[]{:S(2)}) collective-permute-start(bf16[2,80,256]{2,1,0:T(8,128)(2,1)S(1)} %get-tuple-element.48), channel_id=1, source_target_pairs={{3,0},{0,1},{1,2},{2,3},{7,4},{4,5},{5,6},{6,7},{11,8},{8,9},{9,10... | collective-permute-start | bytes 245768 | tf_op jit(solution)/shard_map/ppermute | solution.py:32
  41.3 5.5 %collective-permute-start.3 = (bf16[2,80,256]{2,1,0:T(8,128)(2,1)S(1)}, bf16[2,80,256]{2,1,0:T(8,128)(2,1)S(1)}, u32[]{:S(2)}, u32[]{:S(2)}) collective-permute-start(bf16[2,80,256]{2,1,0:T(8,128)(2,1)S(1)} %get-tuple-element.49), channel_id=1, source_target_pairs={{1,0},{2,1},{3,2},{0,3},{5,4},{6,5},{7,6},{4,7},{9,8},{10,9},{11,1... | collective-permute-start | bytes 245768 | tf_op jit(solution)/shard_map/ppermute | solution.py:32
  43.0 1.2 copy-start.15
  44.2 2.8 %copy-start.2 = (bf16[4,320,480]{2,1,0:T(8,128)(2,1)S(1)}, bf16[4,320,480]{2,1,0:T(8,128)(2,1)}, u32[]{:S(2)}) copy-start(bf16[4,320,480]{2,1,0:T(8,128)(2,1)} %face_ref.5) | copy-start | bytes 3686404
  44.2 2.8 %copy-start.8 = (s32[4,6]{1,0:T(4,128)S(1)}, s32[4,6]{1,0:T(4,128)}, u32[]{:S(2)}) copy-start(s32[4,6]{1,0:T(4,128)} %list_ref.5) | copy-start | bytes 292
  73.1 14.5 %copy-start.16 = (bf16[4,320,320]{2,1,0:T(8,128)(2,1)S(1)}, bf16[4,320,320]{2,1,0:T(8,128)(2,1)}, u32[]{:S(2)}) copy-start(bf16[4,320,320]{2,1,0:T(8,128)(2,1)} %diag_ref.5) | copy-start | bytes 2457604
  82.0 62.2 %copy-start.1 = (f32[1280,256]{1,0:T(8,128)}, f32[1280,256]{1,0:T(8,128)S(1)}, u32[]{:S(2)}) copy-start(f32[1280,256]{1,0:T(8,128)S(1)} %get-tuple-element.62.field_ref.refs_1_.v1_ref) | copy-start | bytes 3932164
  82.0 8.5 %collective-permute-start.4 = (bf16[4,80,256]{2,1,0:T(8,128)(2,1)S(1)}, bf16[4,80,256]{2,1,0:T(8,128)(2,1)S(1)}, u32[]{:S(2)}, u32[]{:S(2)}) collective-permute-start(bf16[4,80,256]{2,1,0:T(8,128)(2,1)S(1)} %get-tuple-element.58), channel_id=1, source_target_pairs={{0,4},{4,8},{8,12},{12,16},{16,20},{20,24},{24,28},{1,5},{5,9},{9,... | collective-permute-start | bytes 491528 | tf_op jit(solution)/shard_map/ppermute | solution.py:26
  84.6 7.6 %collective-permute-start.5 = (bf16[4,80,256]{2,1,0:T(8,128)(2,1)S(1)}, bf16[4,80,256]{2,1,0:T(8,128)(2,1)S(1)}, u32[]{:S(2)}, u32[]{:S(2)}) collective-permute-start(bf16[4,80,256]{2,1,0:T(8,128)(2,1)S(1)} %get-tuple-element.59), channel_id=1, source_target_pairs={{4,0},{8,4},{12,8},{16,12},{20,16},{24,20},{28,24},{5,1},{9,5},{13... | collective-permute-start | bytes 491528 | tf_op jit(solution)/shard_map/ppermute | solution.py:26
  85.9 4.6 %collective-permute-start.6 = (bf16[2,80,256]{2,1,0:T(8,128)(2,1)S(1)}, bf16[2,80,256]{2,1,0:T(8,128)(2,1)S(1)}, u32[]{:S(2)}, u32[]{:S(2)}) collective-permute-start(bf16[2,80,256]{2,1,0:T(8,128)(2,1)S(1)} %get-tuple-element.60), channel_id=1, source_target_pairs={{3,0},{0,1},{1,2},{2,3},{7,4},{4,5},{5,6},{6,7},{11,8},{8,9},{9,10... | collective-permute-start | bytes 245768 | tf_op jit(solution)/shard_map/ppermute | solution.py:32
  85.9 4.6 %collective-permute-start.7 = (bf16[2,80,256]{2,1,0:T(8,128)(2,1)S(1)}, bf16[2,80,256]{2,1,0:T(8,128)(2,1)S(1)}, u32[]{:S(2)}, u32[]{:S(2)}) collective-permute-start(bf16[2,80,256]{2,1,0:T(8,128)(2,1)S(1)} %get-tuple-element.61), channel_id=1, source_target_pairs={{1,0},{2,1},{3,2},{0,3},{5,4},{6,5},{7,6},{4,7},{9,8},{10,9},{11,1... | collective-permute-start | bytes 245768 | tf_op jit(solution)/shard_map/ppermute | solution.py:32
  97.2 27.1 %copy-start.10 = (s32[1,2,4]{2,1,0:T(2,128)S(1)}, s32[1,2,4]{2,1,0:T(2,128)}, u32[]{:S(2)}) copy-start(s32[1,2,4]{2,1,0:T(2,128)} %refs_3_.3) | copy-start | bytes 100
  97.2 27.1 %copy-start.12 = (s32[1,2,2]{2,1,0:T(2,128)S(1)}, s32[1,2,2]{2,1,0:T(2,128)}, u32[]{:S(2)}) copy-start(s32[1,2,2]{2,1,0:T(2,128)} %refs_4_.1) | copy-start | bytes 52
  134.1 10.1 %copy-start.3 = (f32[1280,256]{1,0:T(8,128)}, f32[1280,256]{1,0:T(8,128)S(1)}, u32[]{:S(2)}) copy-start(f32[1280,256]{1,0:T(8,128)S(1)} %get-tuple-element.75.field_ref.refs_2_.v2_ref) | copy-start | bytes 3932164
  134.1 8.9 %collective-permute-start.8 = (bf16[4,80,256]{2,1,0:T(8,128)(2,1)S(1)}, bf16[4,80,256]{2,1,0:T(8,128)(2,1)S(1)}, u32[]{:S(2)}, u32[]{:S(2)}) collective-permute-start(bf16[4,80,256]{2,1,0:T(8,128)(2,1)S(1)} %get-tuple-element.71), channel_id=1, source_target_pairs={{0,4},{4,8},{8,12},{12,16},{16,20},{20,24},{24,28},{1,5},{5,9},{9,... | collective-permute-start | bytes 491528 | tf_op jit(solution)/shard_map/ppermute | solution.py:26
  136.9 7.2 %collective-permute-start.9 = (bf16[4,80,256]{2,1,0:T(8,128)(2,1)S(1)}, bf16[4,80,256]{2,1,0:T(8,128)(2,1)S(1)}, u32[]{:S(2)}, u32[]{:S(2)}) collective-permute-start(bf16[4,80,256]{2,1,0:T(8,128)(2,1)S(1)} %get-tuple-element.72), channel_id=1, source_target_pairs={{4,0},{8,4},{12,8},{16,12},{20,16},{24,20},{28,24},{5,1},{9,5},{13... | collective-permute-start | bytes 491528 | tf_op jit(solution)/shard_map/ppermute | solution.py:26
  138.2 4.8 %collective-permute-start.10 = (bf16[2,80,256]{2,1,0:T(8,128)(2,1)S(1)}, bf16[2,80,256]{2,1,0:T(8,128)(2,1)S(1)}, u32[]{:S(2)}, u32[]{:S(2)}) collective-permute-start(bf16[2,80,256]{2,1,0:T(8,128)(2,1)S(1)} %get-tuple-element.73), channel_id=1, source_target_pairs={{3,0},{0,1},{1,2},{2,3},{7,4},{4,5},{5,6},{6,7},{11,8},{8,9},{9,10... | collective-permute-start | bytes 245768 | tf_op jit(solution)/shard_map/ppermute | solution.py:32
  138.3 4.7 %collective-permute-start.11 = (bf16[2,80,256]{2,1,0:T(8,128)(2,1)S(1)}, bf16[2,80,256]{2,1,0:T(8,128)(2,1)S(1)}, u32[]{:S(2)}, u32[]{:S(2)}) collective-permute-start(bf16[2,80,256]{2,1,0:T(8,128)(2,1)S(1)} %get-tuple-element.74), channel_id=1, source_target_pairs={{1,0},{2,1},{3,2},{0,3},{5,4},{6,5},{7,6},{4,7},{9,8},{10,9},{11,1... | collective-permute-start | bytes 245768 | tf_op jit(solution)/shard_map/ppermute | solution.py:32
  165.6 13.2 %all-to-all-start.7 = ((f32[32,16,128]{2,1,0:T(8,128)}), f32[32,16,128]{2,1,0:T(8,128)S(1)}, u32[]{:S(2)}, u32[]{:S(2)}) async-start(f32[32,16,128]{2,1,0:T(8,128)} %add_up.7), calls=%async_computation.7 | async-start | bytes 524288 | tf_op jit(solution)/shard_map/all_to_all | solution.py:43
  (7 other events, 5.8 us)
where the time goes:
time: 195 us; the launch traced here: 194 us
  blocking collectives  87.2 us (45%)
  Pallas kernels  70.9 us (36%)
  starting transfers between devices  20 us (10%)
  waiting for transfers between devices  7.29 us (4%)
  local copies, waits for them, and re-layouts  6.98 us (4%)
    pallas_call x16, Pallas kernels, call(): pl.pallas_call(kernel, name=name, out_shape=[jax.ShapeDtypeStruct(shape,...  70.9 us
    all_to_all x4, blocking collectives, total(): parts = lax.all_to_all(block.reshape(count, share, width), AXES, 0, 0)  55.3 us
    all_to_all x3, blocking collectives, total(): return lax.all_to_all(mine, AXES, 0, 0).reshape(count * share, width)[:rows]  31.9 us
    ppermute x6, starting transfers between devices, passed_along(): lax.ppermute(value, axis, [(source, source + steps) for source in range(f...  11.8 us
    unnamed x36, local copies, waits for them, and re-layouts  6.98 us
    ppermute x6, starting transfers between devices, shifted(): return lax.ppermute(block, axis, route)  5.37 us
    all_to_all x1, waiting for transfers between devices, total(): return lax.all_to_all(mine, AXES, 0, 0).reshape(count * share, width)[:rows]  4.28 us
  transfers between devices with their start and end apart: 13, of which 4 were waited for; matrix products, arithmetic and copies ran while one was open for 0% of the time, Pallas kernels for 7%

commit v1 on v0

--- a/solution.py
+++ b/solution.py
@@ -34,13 +34,19 @@
 
 def total(block):
     count = lax.axis_size(AXES[0]) * lax.axis_size(AXES[1])
+    if block.ndim == 3:
+        return exchange(block)
     rows, width = block.shape
     share = -(-rows // count)
     if share * count != rows:
         block = jnp.pad(block, ((0, share * count - rows), (0, 0)))
-    parts = lax.all_to_all(block.reshape(count, share, width), AXES, 0, 0)
+    return exchange(block.reshape(count, share, width)).reshape(count * share, width)[:rows]
+
+
+def exchange(shares):
+    parts = lax.all_to_all(shares, AXES, 0, 0)
     (mine,) = call(add_up_kernel, "add_up", [parts], [(parts.shape, F32)], limit=4 * 2**20)
-    return lax.all_to_all(mine, AXES, 0, 0).reshape(count * share, width)[:rows]
+    return lax.all_to_all(mine, AXES, 0, 0)
 
 
 def mm(left, right):
@@ -134,9 +140,54 @@
     return pl.ds(pl.multiple_of(half * width, width), width)
 
 
+def blocks_of(ref, count):
+    if len(ref.shape) == 2:
+        size = ref.shape[-1]
+        return [ref[j * size : (j + 1) * size, :] for j in range(count)]
+    size = ref.shape[-1] // count
+    wide = ref[...].reshape(size, count * size)
+    return [wide[:, j * size : (j + 1) * size] for j in range(count)]
+
+
 def split(value):
     high = value.astype(BF16)
     return high, (value - high.astype(F32)).astype(BF16)
+
+
+def pieces_of(matrix):
+    high, low = split(matrix)
+    both = jnp.concatenate([high, low], 1)
+    return jnp.concatenate([both, both], 0)
+
+
+def mm_pieces(parts, weights):
+    pairs = [split(part) for part in parts]
+    left = jnp.concatenate([p[0] for p in pairs] + [p[1] for p in pairs], 1)
+    out = jnp.dot(left, weights, preferred_element_type=F32)
+    size = out.shape[1] // 2
+    return out[:, :size] + out[:, size:]
+
+
+def thirds_of(matrix):
+    high, low = split(matrix)
+    rest = (matrix - high.astype(F32) - low.astype(F32)).astype(BF16)
+    both = jnp.concatenate([high, low], 1)
+    last = jnp.concatenate([high, jnp.zeros_like(high)], 1)
+    return jnp.concatenate([both, both, last], 0), rest
+
+
+def mm_thirds(parts, weights):
+    weights, rest = weights
+    pairs = [split(part) for part in parts]
+    thirds = [
+        (part - p[0].astype(F32) - p[1].astype(F32)).astype(BF16) for part, p in zip(parts, pairs)
+    ]
+    high = [p[0] for p in pairs]
+    left = jnp.concatenate(high + [p[1] for p in pairs] + thirds, 1)
+    out = jnp.dot(left, weights, preferred_element_type=F32)
+    tail = jnp.dot(jnp.concatenate(high, 1), rest, preferred_element_type=F32)
+    size = out.shape[1] // 2
+    return out[:, :size] + (out[:, size:] + tail)
 
 
 def take_traces(element, rows, picks_ref, field_ref, traces_ref):
@@ -192,11 +243,12 @@
     turn = inverse.T
     first = jnp.concatenate([turn[:half], -turn[half:]], 0)
     second = jnp.concatenate([turn[half:], turn[:half]], 0)
-    wide = jnp.concatenate([first, second], 1)
+    weights = thirds_of(first), thirds_of(second)
 
     @pl.loop(0, count)
     def _(e):
-        field_ref[rows_of(e, rows), :] = mm(rhs_ref[rows_of(e, rows), :], wide)
+        field = [mm_thirds([rhs_ref[rows_of(e, rows), :]], item) for item in weights]
+        field_ref[rows_of(e, rows), :] = jnp.concatenate(field, 1)
         take_traces(e, rows, picks_ref, field_ref, traces_ref)
 
     pack(ssend_ref, traces_ref, (s0_ref, s1_ref))
@@ -209,15 +261,15 @@
     basis = refs[: level + 1]
     picks_ref, ssend_ref, csend_ref = refs[level + 1 : level + 4]
     field_ref, traces_ref, s0_ref, s1_ref, c0_ref, c1_ref, upper_ref, inverse_ref = refs[level + 4 :]
-    width = red_ref.shape[-1]
-    blocks = [red_ref[j * width : (j + 1) * width, :] for j in range(level + 2)]
+    width = image_ref.shape[-1] // 2
+    blocks = blocks_of(red_ref, level + 2)
     coeffs = jnp.concatenate(blocks[:-1], 1)
     gram = blocks[-1] - mm_nt(coeffs, coeffs)
     upper, inverse = factor(gram)
     upper_ref[...] = upper
     inverse_ref[...] = inverse
     turn = inverse.T
-    matrix = jnp.concatenate([turn, -mm_tn(coeffs, turn)], 0)
+    weights = thirds_of(jnp.concatenate([turn, -mm_tn(coeffs, turn)], 0))
     count = traces_ref.shape[0] // FACES
     rows = field_ref.shape[0] // count
 
@@ -227,7 +279,7 @@
         for h in range(2):
             cut = slice(h * width, (h + 1) * width)
             parts = [ref[at, cut] for ref in (image_ref,) + basis]
-            field_ref[at, cut] = mm(jnp.concatenate(parts, 1), matrix)
+            field_ref[at, cut] = mm_thirds(parts, weights)
         take_traces(e, rows, picks_ref, field_ref, traces_ref)
 
     pack(ssend_ref, traces_ref, (s0_ref, s1_ref))
@@ -272,8 +324,8 @@
 ):
     width = s0_ref.shape[0]
     t00 = sums0_ref[:width, :] + shift0_ref[...]
-    t01 = sums1_ref[:width, :]
-    t11 = sums1_ref[width : 2 * width, :] + shift1_ref[...]
+    t01, t11, _ = blocks_of(sums1_ref, 3)
+    t11 = t11 + shift1_ref[...]
     n1 = -mm(i1_ref[...], t00)
     n2 = -mm(i2_ref[...], t01 + mm(t11, n1))
     gram = identity(width) + mm_tn(n1, n1) + mm_tn(n2, n2)
@@ -287,7 +339,7 @@
 def outer_kernel(level, list_ref, traces_ref, prev_ref, next_ref, cprev_ref, cnext_ref,
                  face_ref, part_ref, *refs):
     basis = refs[: level + 1]
-    image_ref, out_ref, table, nearby = refs[level + 1 :]
+    image_ref, out_ref, table, nearby, total_ref = refs[level + 1 :]
     own = traces_ref.shape[0]
     size = traces_ref.shape[1]
     at = 0
@@ -305,7 +357,8 @@
         coupled = jnp.dot(face_ref[e], nearby[...], preferred_element_type=F32)
         image_ref[rows_of(e, rows), :] = part_ref[rows_of(e, rows), :] + coupled
 
-    out_ref[...] = jnp.zeros_like(out_ref)
+    sums_ref = out_ref if len(out_ref.shape) == 2 else total_ref
+    sums_ref[...] = jnp.zeros_like(sums_ref)
     piece = 2 * width if (count * rows) % (2 * width) == 0 else rows
 
     @pl.loop(0, count * rows // piece)
@@ -323,8 +376,14 @@
                 preferred_element_type=F32,
             )
             term = term[:width] + term[width:]
-            for j in range(level + 2):
-                out_ref[j * width : (j + 1) * width, :] += term[:, j * width : (j + 1) * width]
+            if len(out_ref.shape) == 3:
+                sums_ref[...] += term
+            else:
+                for j in range(level + 2):
+                    sums_ref[j * width : (j + 1) * width, :] += term[:, j * width : (j + 1) * width]
+
+    if len(out_ref.shape) == 3:
+        out_ref[...] = sums_ref[...].reshape(out_ref.shape)
 
 
 def final_kernel(
@@ -362,7 +421,7 @@
     rows = []
     for y, w in ((y0, z[0] + hy[0]), (y1, z[1] + hy[1]), (y2, z[2] + hy[2]), (0.0 * y2, -y2)):
         rows.append(jnp.where(left, y, pltpu.roll(w, half, 1)))
-    matrix = jnp.concatenate(rows, 0)
+    weights = pieces_of(jnp.concatenate(rows, 0))
     count = out_sems.shape[1]
     size = solved.shape[0] // count
     lanes = grid_of((size, width), 1) < half
@@ -381,9 +440,7 @@
         at = rows_of(e, size)
 
         cuts = [slice(h * width, (h + 1) * width) for h in range(2)]
-        first, second = [
-            mm(jnp.concatenate([fields[j, at, cut] for j in range(4)], 1), matrix) for cut in cuts
-        ]
+        first, second = [mm_pieces([fields[j, at, cut] for j in range(4)], weights) for cut in cuts]
         solved[at, :] = jnp.where(lanes, first, pltpu.roll(second, half, 1))
         left_over[at, :] = jnp.where(lanes, pltpu.roll(first, half, 1), second)
         for copy in copies(e):
@@ -490,16 +547,22 @@
                 (),
                 10**9,
             )
-        blocks = 2 if step == 0 else 4
+        wide = (blocksize, (step + 2) * blocksize)
+        sums_out = ((step + 2) * blocksize, blocksize)
+        if step == 1:
+            sums_out = (4 * blocksize, blocksize)
+            if blocksize % devices == 0:
+                sums_out = (devices, blocksize // devices, wide[1])
         image, sums = call(
             functools.partial(outer_kernel, step),
             "outer",
             [face_list, traces, from_prev, from_next, cross_prev, cross_next, jac_face, part]
             + basis,
-            [field_out, ((blocks * blocksize, blocksize), F32)],
+            [field_out, (sums_out, F32)],
             [
                 pltpu.VMEM((slots + 2 * ss + 2 * sc + 1, size, columns), BF16),
                 pltpu.VMEM((FACES * size, columns), BF16),
+                pltpu.VMEM(wide, F32),
             ],
             (0,),
         )

time: 195 us -> 187 us (0.959)
  Pallas kernels: 70.9 us -> 65.6 us
  blocking collectives: 87.2 us -> 84.3 us
    pallas_call x16, Pallas kernels: 70.9 us -> 65.6 us  [call(): pl.pallas_call(kernel, name=name, out_shape=[jax.ShapeDtypeStruct(shape,...]
    all_to_all x7, blocking collectives: 87.2 us -> 84.3 us  [the longest x4 53.9 us: exchange(): parts = lax.all_to_all(shares, AXES, 0, 0)]
where the time goes in v1:
time: 187 us; the launch traced here: 186 us
  blocking collectives  84.3 us (45%)
  Pallas kernels  65.6 us (35%)
  starting transfers between devices  19.9 us (11%)
  waiting for transfers between devices  7.45 us (4%)
  local copies, waits for them, and re-layouts  6.97 us (4%)
    pallas_call x16, Pallas kernels, call(): pl.pallas_call(kernel, name=name, out_shape=[jax.ShapeDtypeStruct(shape,...  65.6 us
    all_to_all x4, blocking collectives, exchange(): parts = lax.all_to_all(shares, AXES, 0, 0)  53.9 us
    all_to_all x3, blocking collectives, exchange(): return lax.all_to_all(mine, AXES, 0, 0)  30.4 us
    ppermute x6, starting transfers between devices, passed_along(): lax.ppermute(value, axis, [(source, source + steps) for source in range(f...  11.8 us
    unnamed x36, local copies, waits for them, and re-layouts  6.97 us
    ppermute x6, starting transfers between devices, shifted(): return lax.ppermute(block, axis, route)  5.37 us
    all_to_all x1, waiting for transfers between devices, exchange(): return lax.all_to_all(mine, AXES, 0, 0)  4.27 us
  transfers between devices with their start and end apart: 13, of which 4 were waited for; matrix products, arithmetic and copies ran while one was open for 0% of the time, Pallas kernels for 7%

profile of v1, /device:TPU:0, one launch (start us, length us, event | category | flops | bytes accessed | tf_op | source)
XLA Modules:
  0.0 186.1 jit_solution(11579437826157459440)
XLA Ops:
  3.2 14.5 %all_to_all.40.parts_ref = f32[32,4,128]{2,1,0:T(4,128)S(1)} all-to-all(f32[32,4,128]{2,1,0:T(4,128)S(1)} %bitcast.15), channel_id=1, replica_groups=mesh['stream'=8,'cross'=4] {'stream','cross'}, dimensions={0} | all-to-all | bytes 131072 | tf_op jit(solution)/shard_map/all_to_all | solution.py:47
  17.8 9.1 %all_to_all.41 = f32[32,4,128]{2,1,0:T(4,128)S(1)} all-to-all(f32[32,4,128]{2,1,0:T(4,128)S(1)} %add_up.4), channel_id=1, replica_groups=mesh['stream'=8,'cross'=4] {'stream','cross'}, dimensions={0} | all-to-all | bytes 131072 | tf_op jit(solution)/shard_map/all_to_all | solution.py:49
  28.3 7.3 %start.1 = (f32[1280,256]{1,0:T(8,128)S(1)}, bf16[24,80,256]{2,1,0:T(8,128)(2,1)S(1)}, bf16[4,80,256]{2,1,0:T(8,128)(2,1)S(1)}, bf16[4,80,256]{2,1,0:T(8,128)(2,...) custom-call(f32[128,128]{1,0:T(8,128)S(1)} %bitcast.13, ...), custom_call_target="tpu_custom_call" | custom-call | bytes 1028144 | tf_op jit(solution)/shard_map/start/pallas_call | solution.py:476
  35.6 2.5 %collective-permute-start = (bf16[4,80,256]{2,1,0:T(8,128)(2,1)S(1)}, bf16[4,80,256]{2,1,0:T(8,128)(2,1)S(1)}, u32[]{:S(2)}, u32[]{:S(2)}) collective-permute-start(bf16[4,80,256]{2,1,0:T(8,128)(2,1)S(1)} %get-tuple-element.46), channel_id=1, source_target_pairs={{0,4},{4,8},{8,12},{12,16},{16,20},{20,24},{24,28},{1,5},{5,9},{9,... | collective-permute-start | bytes 491528 | tf_op jit(solution)/shard_map/ppermute | solution.py:26
  43.1 2.5 %inner.3 = (f32[1280,256]{1,0:T(8,128)S(1)}, f32[128,128]{1,0:T(8,128)S(1)}, f32[128,128]{1,0:T(8,128)S(1)}, f32[128,128]{1,0:T(8,128)S(1)}) custom-call(f32[1]{0:T(128)S(6)} %copy.11.omega_ref, f32[8,128]{1,0:T(8,128)S(1)} %get-tuple-element.50.center_ref, f32[4,320]{1,0:T(4,128)S(1)} %copy-done.14, bf16[4,320,320]{2,1,0:T(8,128)(2,1)S(1)} %copy-done.15, ...), custom_call_target="tpu_custom_call" | custom-call | flops 1000000000 | bytes 2270212 | tf_op jit(solution)/shard_map/inner/pallas_call | solution.py:476
  45.9 4.2 %outer.3 = (f32[1280,256]{1,0:T(8,128)S(1)}, f32[256,128]{1,0:T(8,128)S(1)}) custom-call(s32[4,6]{1,0:T(4,128)S(1)} %copy-done.8, bf16[24,80,256]{2,1,0:T(8,128)(2,1)S(1)} %get-tuple-element.45.traces_ref, bf16[4,80,256]{2,1,0:T(8,128)(2,1)S(1)} %collective-permute-done.prev_ref, bf16[4,80,256]{2,1,0:T(8,128)(2,1)S(1)} %collective-permute-done.1.next_ref, ...), custom_call_target="tpu_custom_call" | custom-call | bytes 5324896 | tf_op jit(solution)/shard_map/outer/pallas_call | solution.py:476
  50.1 11.9 %all_to_all.42.parts_ref = f32[32,8,128]{2,1,0:T(8,128)S(1)} all-to-all(f32[32,8,128]{2,1,0:T(8,128)S(1)} %bitcast.16), channel_id=1, replica_groups=mesh['stream'=8,'cross'=4] {'stream','cross'}, dimensions={0} | all-to-all | bytes 262144 | tf_op jit(solution)/shard_map/all_to_all | solution.py:47
  62.1 10.0 %all_to_all.43 = f32[32,8,128]{2,1,0:T(8,128)S(1)} all-to-all(f32[32,8,128]{2,1,0:T(8,128)S(1)} %add_up.5), channel_id=1, replica_groups=mesh['stream'=8,'cross'=4] {'stream','cross'}, dimensions={0} | all-to-all | bytes 262144 | tf_op jit(solution)/shard_map/all_to_all | solution.py:49
  72.0 8.1 %next.2 = (f32[1280,256]{1,0:T(8,128)S(1)}, bf16[24,80,256]{2,1,0:T(8,128)(2,1)S(1)}, bf16[4,80,256]{2,1,0:T(8,128)(2,1)S(1)}, bf16[4,80,256]{2,1,0:T(8,128)(2,1...) custom-call(f32[256,128]{1,0:T(8,128)S(1)} %bitcast.11, ...), custom_call_target="tpu_custom_call" | custom-call | bytes 3059760 | tf_op jit(solution)/shard_map/next/pallas_call | solution.py:476
  80.2 2.6 %collective-permute-start.4 = (bf16[4,80,256]{2,1,0:T(8,128)(2,1)S(1)}, bf16[4,80,256]{2,1,0:T(8,128)(2,1)S(1)}, u32[]{:S(2)}, u32[]{:S(2)}) collective-permute-start(bf16[4,80,256]{2,1,0:T(8,128)(2,1)S(1)} %get-tuple-element.58), channel_id=1, source_target_pairs={{0,4},{4,8},{8,12},{12,16},{16,20},{20,24},{24,28},{1,5},{5,9},{9,... | collective-permute-start | bytes 491528 | tf_op jit(solution)/shard_map/ppermute | solution.py:26
  84.1 1.7 collective-permute-start.7
  85.9 2.8 %inner.4 = (f32[1280,256]{1,0:T(8,128)S(1)}, f32[128,128]{1,0:T(8,128)S(1)}, f32[128,128]{1,0:T(8,128)S(1)}, f32[128,128]{1,0:T(8,128)S(1)}) custom-call(f32[1]{0:T(128)S(6)} %copy.11.omega_ref, f32[8,128]{1,0:T(8,128)S(1)} %get-tuple-element.50.center_ref, f32[4,320]{1,0:T(4,128)S(1)} %copy-done.14, bf16[4,320,320]{2,1,0:T(8,128)(2,1)S(1)} %copy-done.16, ...), custom_call_target="tpu_custom_call" | custom-call | flops 1000000000 | bytes 2401284 | tf_op jit(solution)/shard_map/inner/pallas_call | solution.py:476
  90.4 5.0 %outer.4 = (f32[1280,256]{1,0:T(8,128)S(1)}, f32[32,4,384]{2,1,0:T(4,128)S(1)}) custom-call(s32[4,6]{1,0:T(4,128)S(1)} %copy-done.8, bf16[24,80,256]{2,1,0:T(8,128)(2,1)S(1)} %get-tuple-element.57.traces_ref, bf16[4,80,256]{2,1,0:T(8,128)(2,1)S(1)} %collective-permute-done.4.prev_ref, bf16[4,80,256]{2,1,0:T(8,128)(2,1)S(1)} %collective-permute-done.5.next_ref, ...), custom_call_target="tpu_custom_call" | custom-call | bytes 6635616 | tf_op jit(solution)/shard_map/outer/pallas_call | solution.py:476
  95.4 12.6 %all_to_all.44.parts_ref = f32[32,4,384]{2,1,0:T(4,128)S(1)} all-to-all(f32[32,4,384]{2,1,0:T(4,128)S(1)} %get-tuple-element.68), channel_id=1, replica_groups=mesh['stream'=8,'cross'=4] {'stream','cross'}, dimensions={0} | all-to-all | bytes 393216 | tf_op jit(solution)/shard_map/all_to_all | solution.py:47
  108.1 11.4 %all_to_all.45.red_ref.sums1_ref = f32[32,4,384]{2,1,0:T(4,128)S(1)} all-to-all(f32[32,4,384]{2,1,0:T(4,128)S(1)} %add_up.6), channel_id=1, replica_groups=mesh['stream'=8,'cross'=4] {'stream','cross'}, dimensions={0} | all-to-all | bytes 393216 | tf_op jit(solution)/shard_map/all_to_all | solution.py:49
  119.4 9.1 %next.3 = (f32[1280,256]{1,0:T(8,128)S(1)}, bf16[24,80,256]{2,1,0:T(8,128)(2,1)S(1)}, bf16[4,80,256]{2,1,0:T(8,128)(2,1)S(1)}, bf16[4,80,256]{2,1,0:T(8,128)(2,1...) custom-call(f32[32,4,384]{2,1,0:T(4,128)S(1)} %all_to_all.45.red_ref, ...), custom_call_target="tpu_custom_call" | custom-call | bytes 4436016 | tf_op jit(solution)/shard_map/next/pallas_call | solution.py:476
  128.6 2.8 %collective-permute-start.8 = (bf16[4,80,256]{2,1,0:T(8,128)(2,1)S(1)}, bf16[4,80,256]{2,1,0:T(8,128)(2,1)S(1)}, u32[]{:S(2)}, u32[]{:S(2)}) collective-permute-start(bf16[4,80,256]{2,1,0:T(8,128)(2,1)S(1)} %get-tuple-element.71), channel_id=1, source_target_pairs={{0,4},{4,8},{8,12},{12,16},{16,20},{20,24},{24,28},{1,5},{5,9},{9,... | collective-permute-start | bytes 491528 | tf_op jit(solution)/shard_map/ppermute | solution.py:26
  134.5 3.0 %inner.5 = (f32[1280,256]{1,0:T(8,128)S(1)}, f32[128,128]{1,0:T(8,128)S(1)}, f32[128,128]{1,0:T(8,128)}, f32[128,128]{1,0:T(8,128)}) custom-call(f32[1]{0:T(128)S(6)} %copy.11.omega_ref, f32[8,128]{1,0:T(8,128)S(1)} %get-tuple-element.50.center_ref, f32[4,320]{1,0:T(4,128)S(1)} %copy-done.14, bf16[4,320,320]{2,1,0:T(8,128)(2,1)S(1)} %copy-done.16, ...), custom_call_target="tpu_custom_call" | custom-call | flops 1000000000 | bytes 2401284 | tf_op jit(solution)/shard_map/inner/pallas_call | solution.py:476
  138.8 5.0 %outer.5 = (f32[1280,256]{1,0:T(8,128)S(1)}, f32[512,128]{1,0:T(8,128)S(1)}) custom-call(s32[4,6]{1,0:T(4,128)S(1)} %copy-done.8, bf16[24,80,256]{2,1,0:T(8,128)(2,1)S(1)} %get-tuple-element.70.traces_ref, bf16[4,80,256]{2,1,0:T(8,128)(2,1)S(1)} %collective-permute-done.8.prev_ref, bf16[4,80,256]{2,1,0:T(8,128)(2,1)S(1)} %collective-permute-done.9.next_ref, ...), custom_call_target="tpu_custom_call" | custom-call | bytes 7946336 | tf_op jit(solution)/shard_map/outer/pallas_call | solution.py:476
  144.8 14.8 %all_to_all.46.parts_ref = f32[32,16,128]{2,1,0:T(8,128)S(1)} all-to-all(f32[32,16,128]{2,1,0:T(8,128)S(1)} %bitcast.14), channel_id=1, replica_groups=mesh['stream'=8,'cross'=4] {'stream','cross'}, dimensions={0} | all-to-all | bytes 524288 | tf_op jit(solution)/shard_map/all_to_all | solution.py:47
  160.4 2.8 %all-to-all-start.7 = ((f32[32,16,128]{2,1,0:T(8,128)}), f32[32,16,128]{2,1,0:T(8,128)S(1)}, u32[]{:S(2)}, u32[]{:S(2)}) async-start(f32[32,16,128]{2,1,0:T(8,128)} %add_up.7), calls=%async_computation.7 | async-start | bytes 524288 | tf_op jit(solution)/shard_map/all_to_all | solution.py:49
  163.2 5.3 %square.1.pack_ref = f32[8,128,128]{2,1,0:T(8,128)S(1)} custom-call(f32[256,128]{1,0:T(8,128)S(1)} %bitcast.12, f32[32,4,384]{2,1,0:T(4,128)S(1)} %all_to_all.45.red_ref.sums1_ref, f32[128,128]{1,0:T(8,128)S(1)} %get-tuple-element.83.shift0_ref, f32[128,128]{1,0:T(8,128)S(1)} %get-tuple-element.84.shift1_ref, f32[128,128]{1,0:T(8,128)S(1)} %get-tuple-element.85.shift2_ref, ...), custom_call_target="tpu_custom_call" | custom-call | flops 1000000000 | bytes 720896 | tf_op jit(solution)/shard_map/square/pallas_call | solution.py:476
  169.3 4.3 %all-to-all-done.7 = f32[32,16,128]{2,1,0:T(8,128)S(1)} async-done(((f32[32,16,128]{2,1,0:T(8,128)}), f32[32,16,128]{2,1,0:T(8,128)S(1)}, u32[]{:S(2)}, u32[]{:S(2)}) %all-to-all-start.7) | async-done | bytes 262176 | tf_op jit(solution)/shard_map/all_to_all | solution.py:49
  174.3 11.6 %final.1 = (f32[1280,128]{1,0:T(8,128)}, f32[1280,128]{1,0:T(8,128)}) custom-call(f32[512,128]{1,0:T(8,128)} %bitcast.17, f32[1280,256]{1,0:T(8,128)} %copy-done.6, f32[1280,256]{1,0:T(8,128)} %copy-done, f32[1280,256]{1,0:T(8,128)} %copy-done.1, f32[1280,256]{1,0:T(8,128)} %copy-done.3, f32[8,128,128]{2,1,0:T(8,128)} %copy-done.7), custom_call_target="tpu_custom_call" | custom-call | bytes 6029312 | tf_op jit(solution)/shard_map/final/pallas_call | solution.py:476
  (61 shorter events, 19.3 us)
Async XLA Ops:
  0.6 26.3 %copy-start.4 = (bf16[480,320]{1,0:T(8,128)(2,1)S(1)}, bf16[480,320]{1,0:T(8,128)(2,1)}, u32[]{:S(2)}) copy-start(bf16[480,320]{1,0:T(8,128)(2,1)} %constant.2.clone.picks_ref.refs_1_.refs_2_) | copy-start | bytes 921604
  2.5 39.4 %copy-start.14 = (f32[4,320]{1,0:T(4,128)S(1)}, f32[4,320]{1,0:T(4,128)}, u32[]{:S(2)}) copy-start(f32[4,320]{1,0:T(4,128)} %damping_ref.7) | copy-start | bytes 15364
  35.6 103.2 %copy-start = (f32[1280,256]{1,0:T(8,128)}, f32[1280,256]{1,0:T(8,128)S(1)}, u32[]{:S(2)}) copy-start(f32[1280,256]{1,0:T(8,128)S(1)} %get-tuple-element.51.field_ref.refs_0_.v0_ref) | copy-start | bytes 3932164
  35.6 10.1 %collective-permute-start = (bf16[4,80,256]{2,1,0:T(8,128)(2,1)S(1)}, bf16[4,80,256]{2,1,0:T(8,128)(2,1)S(1)}, u32[]{:S(2)}, u32[]{:S(2)}) collective-permute-start(bf16[4,80,256]{2,1,0:T(8,128)(2,1)S(1)} %get-tuple-element.46), channel_id=1, source_target_pairs={{0,4},{4,8},{8,12},{12,16},{16,20},{20,24},{24,28},{1,5},{5,9},{9,... | collective-permute-start | bytes 491528 | tf_op jit(solution)/shard_map/ppermute | solution.py:26
  38.1 7.7 %collective-permute-start.1 = (bf16[4,80,256]{2,1,0:T(8,128)(2,1)S(1)}, bf16[4,80,256]{2,1,0:T(8,128)(2,1)S(1)}, u32[]{:S(2)}, u32[]{:S(2)}) collective-permute-start(bf16[4,80,256]{2,1,0:T(8,128)(2,1)S(1)} %get-tuple-element.47), channel_id=1, source_target_pairs={{4,0},{8,4},{12,8},{16,12},{20,16},{24,20},{28,24},{5,1},{9,5},{13... | collective-permute-start | bytes 491528 | tf_op jit(solution)/shard_map/ppermute | solution.py:26
  40.1 5.6 %collective-permute-start.2 = (bf16[2,80,256]{2,1,0:T(8,128)(2,1)S(1)}, bf16[2,80,256]{2,1,0:T(8,128)(2,1)S(1)}, u32[]{:S(2)}, u32[]{:S(2)}) collective-permute-start(bf16[2,80,256]{2,1,0:T(8,128)(2,1)S(1)} %get-tuple-element.48), channel_id=1, source_target_pairs={{3,0},{0,1},{1,2},{2,3},{7,4},{4,5},{5,6},{6,7},{11,8},{8,9},{9,10... | collective-permute-start | bytes 245768 | tf_op jit(solution)/shard_map/ppermute | solution.py:32
  40.1 5.5 %collective-permute-start.3 = (bf16[2,80,256]{2,1,0:T(8,128)(2,1)S(1)}, bf16[2,80,256]{2,1,0:T(8,128)(2,1)S(1)}, u32[]{:S(2)}, u32[]{:S(2)}) collective-permute-start(bf16[2,80,256]{2,1,0:T(8,128)(2,1)S(1)} %get-tuple-element.49), channel_id=1, source_target_pairs={{1,0},{2,1},{3,2},{0,3},{5,4},{6,5},{7,6},{4,7},{9,8},{10,9},{11,1... | collective-permute-start | bytes 245768 | tf_op jit(solution)/shard_map/ppermute | solution.py:32
  41.9 1.2 copy-start.15
  43.1 2.8 %copy-start.2 = (bf16[4,320,480]{2,1,0:T(8,128)(2,1)S(1)}, bf16[4,320,480]{2,1,0:T(8,128)(2,1)}, u32[]{:S(2)}) copy-start(bf16[4,320,480]{2,1,0:T(8,128)(2,1)} %face_ref.5) | copy-start | bytes 3686404
  43.1 2.8 %copy-start.8 = (s32[4,6]{1,0:T(4,128)S(1)}, s32[4,6]{1,0:T(4,128)}, u32[]{:S(2)}) copy-start(s32[4,6]{1,0:T(4,128)} %list_ref.5) | copy-start | bytes 292
  72.0 13.9 %copy-start.16 = (bf16[4,320,320]{2,1,0:T(8,128)(2,1)S(1)}, bf16[4,320,320]{2,1,0:T(8,128)(2,1)}, u32[]{:S(2)}) copy-start(bf16[4,320,320]{2,1,0:T(8,128)(2,1)} %diag_ref.5) | copy-start | bytes 2457604
  80.2 58.6 %copy-start.1 = (f32[1280,256]{1,0:T(8,128)}, f32[1280,256]{1,0:T(8,128)S(1)}, u32[]{:S(2)}) copy-start(f32[1280,256]{1,0:T(8,128)S(1)} %get-tuple-element.62.field_ref.refs_1_.v1_ref) | copy-start | bytes 3932164
  80.2 8.6 %collective-permute-start.4 = (bf16[4,80,256]{2,1,0:T(8,128)(2,1)S(1)}, bf16[4,80,256]{2,1,0:T(8,128)(2,1)S(1)}, u32[]{:S(2)}, u32[]{:S(2)}) collective-permute-start(bf16[4,80,256]{2,1,0:T(8,128)(2,1)S(1)} %get-tuple-element.58), channel_id=1, source_target_pairs={{0,4},{4,8},{8,12},{12,16},{16,20},{20,24},{24,28},{1,5},{5,9},{9,... | collective-permute-start | bytes 491528 | tf_op jit(solution)/shard_map/ppermute | solution.py:26
  82.8 7.6 %collective-permute-start.5 = (bf16[4,80,256]{2,1,0:T(8,128)(2,1)S(1)}, bf16[4,80,256]{2,1,0:T(8,128)(2,1)S(1)}, u32[]{:S(2)}, u32[]{:S(2)}) collective-permute-start(bf16[4,80,256]{2,1,0:T(8,128)(2,1)S(1)} %get-tuple-element.59), channel_id=1, source_target_pairs={{4,0},{8,4},{12,8},{16,12},{20,16},{24,20},{28,24},{5,1},{9,5},{13... | collective-permute-start | bytes 491528 | tf_op jit(solution)/shard_map/ppermute | solution.py:26
  84.1 4.6 %collective-permute-start.6 = (bf16[2,80,256]{2,1,0:T(8,128)(2,1)S(1)}, bf16[2,80,256]{2,1,0:T(8,128)(2,1)S(1)}, u32[]{:S(2)}, u32[]{:S(2)}) collective-permute-start(bf16[2,80,256]{2,1,0:T(8,128)(2,1)S(1)} %get-tuple-element.60), channel_id=1, source_target_pairs={{3,0},{0,1},{1,2},{2,3},{7,4},{4,5},{5,6},{6,7},{11,8},{8,9},{9,10... | collective-permute-start | bytes 245768 | tf_op jit(solution)/shard_map/ppermute | solution.py:32
  84.1 4.6 %collective-permute-start.7 = (bf16[2,80,256]{2,1,0:T(8,128)(2,1)S(1)}, bf16[2,80,256]{2,1,0:T(8,128)(2,1)S(1)}, u32[]{:S(2)}, u32[]{:S(2)}) collective-permute-start(bf16[2,80,256]{2,1,0:T(8,128)(2,1)S(1)} %get-tuple-element.61), channel_id=1, source_target_pairs={{1,0},{2,1},{3,2},{0,3},{5,4},{6,5},{7,6},{4,7},{9,8},{10,9},{11,1... | collective-permute-start | bytes 245768 | tf_op jit(solution)/shard_map/ppermute | solution.py:32
  90.4 29.0 %copy-start.10 = (s32[1,2,4]{2,1,0:T(2,128)S(1)}, s32[1,2,4]{2,1,0:T(2,128)}, u32[]{:S(2)}) copy-start(s32[1,2,4]{2,1,0:T(2,128)} %refs_3_.3) | copy-start | bytes 100
  90.4 29.0 %copy-start.12 = (s32[1,2,2]{2,1,0:T(2,128)S(1)}, s32[1,2,2]{2,1,0:T(2,128)}, u32[]{:S(2)}) copy-start(s32[1,2,2]{2,1,0:T(2,128)} %refs_4_.1) | copy-start | bytes 52
  128.6 10.2 %copy-start.3 = (f32[1280,256]{1,0:T(8,128)}, f32[1280,256]{1,0:T(8,128)S(1)}, u32[]{:S(2)}) copy-start(f32[1280,256]{1,0:T(8,128)S(1)} %get-tuple-element.75.field_ref.refs_2_.v2_ref) | copy-start | bytes 3932164
  128.6 8.9 %collective-permute-start.8 = (bf16[4,80,256]{2,1,0:T(8,128)(2,1)S(1)}, bf16[4,80,256]{2,1,0:T(8,128)(2,1)S(1)}, u32[]{:S(2)}, u32[]{:S(2)}) collective-permute-start(bf16[4,80,256]{2,1,0:T(8,128)(2,1)S(1)} %get-tuple-element.71), channel_id=1, source_target_pairs={{0,4},{4,8},{8,12},{12,16},{16,20},{20,24},{24,28},{1,5},{5,9},{9,... | collective-permute-start | bytes 491528 | tf_op jit(solution)/shard_map/ppermute | solution.py:26
  131.4 7.4 %collective-permute-start.9 = (bf16[4,80,256]{2,1,0:T(8,128)(2,1)S(1)}, bf16[4,80,256]{2,1,0:T(8,128)(2,1)S(1)}, u32[]{:S(2)}, u32[]{:S(2)}) collective-permute-start(bf16[4,80,256]{2,1,0:T(8,128)(2,1)S(1)} %get-tuple-element.72), channel_id=1, source_target_pairs={{4,0},{8,4},{12,8},{16,12},{20,16},{24,20},{28,24},{5,1},{9,5},{13... | collective-permute-start | bytes 491528 | tf_op jit(solution)/shard_map/ppermute | solution.py:26
  132.7 4.8 %collective-permute-start.10 = (bf16[2,80,256]{2,1,0:T(8,128)(2,1)S(1)}, bf16[2,80,256]{2,1,0:T(8,128)(2,1)S(1)}, u32[]{:S(2)}, u32[]{:S(2)}) collective-permute-start(bf16[2,80,256]{2,1,0:T(8,128)(2,1)S(1)} %get-tuple-element.73), channel_id=1, source_target_pairs={{3,0},{0,1},{1,2},{2,3},{7,4},{4,5},{5,6},{6,7},{11,8},{8,9},{9,10... | collective-permute-start | bytes 245768 | tf_op jit(solution)/shard_map/ppermute | solution.py:32
  132.7 4.7 %collective-permute-start.11 = (bf16[2,80,256]{2,1,0:T(8,128)(2,1)S(1)}, bf16[2,80,256]{2,1,0:T(8,128)(2,1)S(1)}, u32[]{:S(2)}, u32[]{:S(2)}) collective-permute-start(bf16[2,80,256]{2,1,0:T(8,128)(2,1)S(1)} %get-tuple-element.74), channel_id=1, source_target_pairs={{1,0},{2,1},{3,2},{0,3},{5,4},{6,5},{7,6},{4,7},{9,8},{10,9},{11,1... | collective-permute-start | bytes 245768 | tf_op jit(solution)/shard_map/ppermute | solution.py:32
  160.4 13.2 %all-to-all-start.7 = ((f32[32,16,128]{2,1,0:T(8,128)}), f32[32,16,128]{2,1,0:T(8,128)S(1)}, u32[]{:S(2)}, u32[]{:S(2)}) async-start(f32[32,16,128]{2,1,0:T(8,128)} %add_up.7), calls=%async_computation.7 | async-start | bytes 524288 | tf_op jit(solution)/shard_map/all_to_all | solution.py:49
  (7 other events, 5.8 us)

commit v2 on v1

--- a/solution.py
+++ b/solution.py
@@ -209,9 +209,11 @@
 
 
 def start_gram_kernel(rhs_ref, damping_ref, out_ref):
-    field = rhs_ref[...]
-    width = field.shape[-1]
-    gram = mm_tn(field, field)
+    width = rhs_ref.shape[-1]
+    both = jnp.concatenate(split(rhs_ref[...]), 1)
+    gram = lax.dot_general(both, both, (((0,), (0,)), ((), ())), preferred_element_type=F32)
+    gram = gram[:width] + gram[width:]
+    gram = gram[:, :width] + gram[:, width:]
     mass = jnp.sum(jnp.sum(damping_ref[...], axis=1, keepdims=True), axis=0, keepdims=True)
     corner = (grid_of(gram.shape, 0) == width - 1) & (grid_of(gram.shape, 1) == 0)
     out_ref[...] = jnp.where(corner, mass, gram)
@@ -363,24 +365,24 @@
 
     @pl.loop(0, count * rows // piece)
     def _(i):
-        @pl.loop(0, 2)
-        def _(h):
-            at = (rows_of(i, piece), lanes_of(h, width))
+        lefts, rights = [], []
+        for h in range(2):
+            at = (rows_of(i, piece), slice(h * width, (h + 1) * width))
             parts = [split(ref[at]) for ref in basis + (image_ref,)]
-            left = jnp.concatenate(parts[-1], 1)
-            right = jnp.concatenate([jnp.concatenate([p[k] for p in parts], 1) for k in range(2)], 0)
-            term = lax.dot_general(
-                jnp.concatenate([left, left], 0),
-                right,
-                (((0,), (0,)), ((), ())),
-                preferred_element_type=F32,
-            )
-            term = term[:width] + term[width:]
-            if len(out_ref.shape) == 3:
-                sums_ref[...] += term
-            else:
-                for j in range(level + 2):
-                    sums_ref[j * width : (j + 1) * width, :] += term[:, j * width : (j + 1) * width]
+            lefts += [jnp.concatenate(parts[-1], 1)] * 2
+            rights += [jnp.concatenate([p[k] for p in parts], 1) for k in range(2)]
+        term = lax.dot_general(
+            jnp.concatenate(lefts, 0),
+            jnp.concatenate(rights, 0),
+            (((0,), (0,)), ((), ())),
+            preferred_element_type=F32,
+        )
+        term = term[:width] + term[width:]
+        if len(out_ref.shape) == 3:
+            sums_ref[...] += term
+        else:
+            for j in range(level + 2):
+                sums_ref[j * width : (j + 1) * width, :] += term[:, j * width : (j + 1) * width]
 
     if len(out_ref.shape) == 3:
         out_ref[...] = sums_ref[...].reshape(out_ref.shape)

time: 187 us -> 184 us (0.984)
  Pallas kernels: 65.6 us -> 62.6 us
    pallas_call x16, Pallas kernels: 65.6 us -> 62.6 us  [call(): pl.pallas_call(kernel, name=name, out_shape=[jax.ShapeDtypeStruct(shape,...]
where the time goes in v2:
time: 184 us; the launch traced here: 183 us
  blocking collectives  84.3 us (46%)
  Pallas kernels  62.6 us (34%)
  starting transfers between devices  19.9 us (11%)
  waiting for transfers between devices  7.45 us (4%)
  local copies, waits for them, and re-layouts  6.97 us (4%)
    pallas_call x16, Pallas kernels, call(): pl.pallas_call(kernel, name=name, out_shape=[jax.ShapeDtypeStruct(shape,...  62.6 us
    all_to_all x4, blocking collectives, exchange(): parts = lax.all_to_all(shares, AXES, 0, 0)  53.9 us
    all_to_all x3, blocking collectives, exchange(): return lax.all_to_all(mine, AXES, 0, 0)  30.4 us
    ppermute x6, starting transfers between devices, passed_along(): lax.ppermute(value, axis, [(source, source + steps) for source in range(f...  11.8 us
    unnamed x36, local copies, waits for them, and re-layouts  6.97 us
    ppermute x6, starting transfers between devices, shifted(): return lax.ppermute(block, axis, route)  5.37 us
    all_to_all x1, waiting for transfers between devices, exchange(): return lax.all_to_all(mine, AXES, 0, 0)  4.27 us
  transfers between devices with their start and end apart: 13, of which 4 were waited for; matrix products, arithmetic and copies ran while one was open for 0% of the time, Pallas kernels for 7%

profile of v2, /device:TPU:0, one launch (start us, length us, event | category | flops | bytes accessed | tf_op | source)
XLA Modules:
  0.0 183.1 jit_solution(9391615579540092469)
XLA Ops:
  2.9 14.5 %all_to_all.40.parts_ref = f32[32,4,128]{2,1,0:T(4,128)S(1)} all-to-all(f32[32,4,128]{2,1,0:T(4,128)S(1)} %bitcast.15), channel_id=1, replica_groups=mesh['stream'=8,'cross'=4] {'stream','cross'}, dimensions={0} | all-to-all | bytes 131072 | tf_op jit(solution)/shard_map/all_to_all | solution.py:47
  17.4 9.1 %all_to_all.41 = f32[32,4,128]{2,1,0:T(4,128)S(1)} all-to-all(f32[32,4,128]{2,1,0:T(4,128)S(1)} %add_up.4), channel_id=1, replica_groups=mesh['stream'=8,'cross'=4] {'stream','cross'}, dimensions={0} | all-to-all | bytes 131072 | tf_op jit(solution)/shard_map/all_to_all | solution.py:49
  27.9 7.3 %start.1 = (f32[1280,256]{1,0:T(8,128)S(1)}, bf16[24,80,256]{2,1,0:T(8,128)(2,1)S(1)}, bf16[4,80,256]{2,1,0:T(8,128)(2,1)S(1)}, bf16[4,80,256]{2,1,0:T(8,128)(2,...) custom-call(f32[128,128]{1,0:T(8,128)S(1)} %bitcast.13, ...), custom_call_target="tpu_custom_call" | custom-call | bytes 1028144 | tf_op jit(solution)/shard_map/start/pallas_call | solution.py:478
  35.2 2.5 %collective-permute-start = (bf16[4,80,256]{2,1,0:T(8,128)(2,1)S(1)}, bf16[4,80,256]{2,1,0:T(8,128)(2,1)S(1)}, u32[]{:S(2)}, u32[]{:S(2)}) collective-permute-start(bf16[4,80,256]{2,1,0:T(8,128)(2,1)S(1)} %get-tuple-element.46), channel_id=1, source_target_pairs={{0,4},{4,8},{8,12},{12,16},{16,20},{20,24},{24,28},{1,5},{5,9},{9,... | collective-permute-start | bytes 491528 | tf_op jit(solution)/shard_map/ppermute | solution.py:26
  42.7 2.5 %inner.3 = (f32[1280,256]{1,0:T(8,128)S(1)}, f32[128,128]{1,0:T(8,128)S(1)}, f32[128,128]{1,0:T(8,128)S(1)}, f32[128,128]{1,0:T(8,128)S(1)}) custom-call(f32[1]{0:T(128)S(6)} %copy.11.omega_ref, f32[8,128]{1,0:T(8,128)S(1)} %get-tuple-element.50.center_ref, f32[4,320]{1,0:T(4,128)S(1)} %copy-done.14, bf16[4,320,320]{2,1,0:T(8,128)(2,1)S(1)} %copy-done.15, ...), custom_call_target="tpu_custom_call" | custom-call | flops 1000000000 | bytes 2270212 | tf_op jit(solution)/shard_map/inner/pallas_call | solution.py:478
  45.5 3.4 %outer.3 = (f32[1280,256]{1,0:T(8,128)S(1)}, f32[256,128]{1,0:T(8,128)S(1)}) custom-call(s32[4,6]{1,0:T(4,128)S(1)} %copy-done.8, bf16[24,80,256]{2,1,0:T(8,128)(2,1)S(1)} %get-tuple-element.45.traces_ref, bf16[4,80,256]{2,1,0:T(8,128)(2,1)S(1)} %collective-permute-done.prev_ref, bf16[4,80,256]{2,1,0:T(8,128)(2,1)S(1)} %collective-permute-done.1.next_ref, ...), custom_call_target="tpu_custom_call" | custom-call | bytes 5324896 | tf_op jit(solution)/shard_map/outer/pallas_call | solution.py:478
  48.9 11.9 %all_to_all.42.parts_ref = f32[32,8,128]{2,1,0:T(8,128)S(1)} all-to-all(f32[32,8,128]{2,1,0:T(8,128)S(1)} %bitcast.16), channel_id=1, replica_groups=mesh['stream'=8,'cross'=4] {'stream','cross'}, dimensions={0} | all-to-all | bytes 262144 | tf_op jit(solution)/shard_map/all_to_all | solution.py:47
  60.9 10.0 %all_to_all.43 = f32[32,8,128]{2,1,0:T(8,128)S(1)} all-to-all(f32[32,8,128]{2,1,0:T(8,128)S(1)} %add_up.5), channel_id=1, replica_groups=mesh['stream'=8,'cross'=4] {'stream','cross'}, dimensions={0} | all-to-all | bytes 262144 | tf_op jit(solution)/shard_map/all_to_all | solution.py:49
  70.9 8.1 %next.2 = (f32[1280,256]{1,0:T(8,128)S(1)}, bf16[24,80,256]{2,1,0:T(8,128)(2,1)S(1)}, bf16[4,80,256]{2,1,0:T(8,128)(2,1)S(1)}, bf16[4,80,256]{2,1,0:T(8,128)(2,1...) custom-call(f32[256,128]{1,0:T(8,128)S(1)} %bitcast.11, ...), custom_call_target="tpu_custom_call" | custom-call | bytes 3059760 | tf_op jit(solution)/shard_map/next/pallas_call | solution.py:478
  79.0 2.6 %collective-permute-start.4 = (bf16[4,80,256]{2,1,0:T(8,128)(2,1)S(1)}, bf16[4,80,256]{2,1,0:T(8,128)(2,1)S(1)}, u32[]{:S(2)}, u32[]{:S(2)}) collective-permute-start(bf16[4,80,256]{2,1,0:T(8,128)(2,1)S(1)} %get-tuple-element.58), channel_id=1, source_target_pairs={{0,4},{4,8},{8,12},{12,16},{16,20},{20,24},{24,28},{1,5},{5,9},{9,... | collective-permute-start | bytes 491528 | tf_op jit(solution)/shard_map/ppermute | solution.py:26
  83.0 1.7 collective-permute-start.7
  84.7 2.8 %inner.4 = (f32[1280,256]{1,0:T(8,128)S(1)}, f32[128,128]{1,0:T(8,128)S(1)}, f32[128,128]{1,0:T(8,128)S(1)}, f32[128,128]{1,0:T(8,128)S(1)}) custom-call(f32[1]{0:T(128)S(6)} %copy.11.omega_ref, f32[8,128]{1,0:T(8,128)S(1)} %get-tuple-element.50.center_ref, f32[4,320]{1,0:T(4,128)S(1)} %copy-done.14, bf16[4,320,320]{2,1,0:T(8,128)(2,1)S(1)} %copy-done.16, ...), custom_call_target="tpu_custom_call" | custom-call | flops 1000000000 | bytes 2401284 | tf_op jit(solution)/shard_map/inner/pallas_call | solution.py:478
  89.2 4.1 %outer.4 = (f32[1280,256]{1,0:T(8,128)S(1)}, f32[32,4,384]{2,1,0:T(4,128)S(1)}) custom-call(s32[4,6]{1,0:T(4,128)S(1)} %copy-done.8, bf16[24,80,256]{2,1,0:T(8,128)(2,1)S(1)} %get-tuple-element.57.traces_ref, bf16[4,80,256]{2,1,0:T(8,128)(2,1)S(1)} %collective-permute-done.4.prev_ref, bf16[4,80,256]{2,1,0:T(8,128)(2,1)S(1)} %collective-permute-done.5.next_ref, ...), custom_call_target="tpu_custom_call" | custom-call | bytes 6635616 | tf_op jit(solution)/shard_map/outer/pallas_call | solution.py:478
  93.3 12.6 %all_to_all.44.parts_ref = f32[32,4,384]{2,1,0:T(4,128)S(1)} all-to-all(f32[32,4,384]{2,1,0:T(4,128)S(1)} %get-tuple-element.68), channel_id=1, replica_groups=mesh['stream'=8,'cross'=4] {'stream','cross'}, dimensions={0} | all-to-all | bytes 393216 | tf_op jit(solution)/shard_map/all_to_all | solution.py:47
  106.0 11.4 %all_to_all.45.red_ref.sums1_ref = f32[32,4,384]{2,1,0:T(4,128)S(1)} all-to-all(f32[32,4,384]{2,1,0:T(4,128)S(1)} %add_up.6), channel_id=1, replica_groups=mesh['stream'=8,'cross'=4] {'stream','cross'}, dimensions={0} | all-to-all | bytes 393216 | tf_op jit(solution)/shard_map/all_to_all | solution.py:49
  117.3 9.1 %next.3 = (f32[1280,256]{1,0:T(8,128)S(1)}, bf16[24,80,256]{2,1,0:T(8,128)(2,1)S(1)}, bf16[4,80,256]{2,1,0:T(8,128)(2,1)S(1)}, bf16[4,80,256]{2,1,0:T(8,128)(2,1...) custom-call(f32[32,4,384]{2,1,0:T(4,128)S(1)} %all_to_all.45.red_ref, ...), custom_call_target="tpu_custom_call" | custom-call | bytes 4436016 | tf_op jit(solution)/shard_map/next/pallas_call | solution.py:478
  126.5 2.8 %collective-permute-start.8 = (bf16[4,80,256]{2,1,0:T(8,128)(2,1)S(1)}, bf16[4,80,256]{2,1,0:T(8,128)(2,1)S(1)}, u32[]{:S(2)}, u32[]{:S(2)}) collective-permute-start(bf16[4,80,256]{2,1,0:T(8,128)(2,1)S(1)} %get-tuple-element.71), channel_id=1, source_target_pairs={{0,4},{4,8},{8,12},{12,16},{16,20},{20,24},{24,28},{1,5},{5,9},{9,... | collective-permute-start | bytes 491528 | tf_op jit(solution)/shard_map/ppermute | solution.py:26
  132.4 3.0 %inner.5 = (f32[1280,256]{1,0:T(8,128)S(1)}, f32[128,128]{1,0:T(8,128)S(1)}, f32[128,128]{1,0:T(8,128)}, f32[128,128]{1,0:T(8,128)}) custom-call(f32[1]{0:T(128)S(6)} %copy.11.omega_ref, f32[8,128]{1,0:T(8,128)S(1)} %get-tuple-element.50.center_ref, f32[4,320]{1,0:T(4,128)S(1)} %copy-done.14, bf16[4,320,320]{2,1,0:T(8,128)(2,1)S(1)} %copy-done.16, ...), custom_call_target="tpu_custom_call" | custom-call | flops 1000000000 | bytes 2401284 | tf_op jit(solution)/shard_map/inner/pallas_call | solution.py:478
  136.7 4.1 %outer.5 = (f32[1280,256]{1,0:T(8,128)S(1)}, f32[512,128]{1,0:T(8,128)S(1)}) custom-call(s32[4,6]{1,0:T(4,128)S(1)} %copy-done.8, bf16[24,80,256]{2,1,0:T(8,128)(2,1)S(1)} %get-tuple-element.70.traces_ref, bf16[4,80,256]{2,1,0:T(8,128)(2,1)S(1)} %collective-permute-done.8.prev_ref, bf16[4,80,256]{2,1,0:T(8,128)(2,1)S(1)} %collective-permute-done.9.next_ref, ...), custom_call_target="tpu_custom_call" | custom-call | bytes 7946336 | tf_op jit(solution)/shard_map/outer/pallas_call | solution.py:478
  141.8 14.8 %all_to_all.46.parts_ref = f32[32,16,128]{2,1,0:T(8,128)S(1)} all-to-all(f32[32,16,128]{2,1,0:T(8,128)S(1)} %bitcast.14), channel_id=1, replica_groups=mesh['stream'=8,'cross'=4] {'stream','cross'}, dimensions={0} | all-to-all | bytes 524288 | tf_op jit(solution)/shard_map/all_to_all | solution.py:47
  157.4 2.8 %all-to-all-start.7 = ((f32[32,16,128]{2,1,0:T(8,128)}), f32[32,16,128]{2,1,0:T(8,128)S(1)}, u32[]{:S(2)}, u32[]{:S(2)}) async-start(f32[32,16,128]{2,1,0:T(8,128)} %add_up.7), calls=%async_computation.7 | async-start | bytes 524288 | tf_op jit(solution)/shard_map/all_to_all | solution.py:49
  160.3 5.3 %square.1.pack_ref = f32[8,128,128]{2,1,0:T(8,128)S(1)} custom-call(f32[256,128]{1,0:T(8,128)S(1)} %bitcast.12, f32[32,4,384]{2,1,0:T(4,128)S(1)} %all_to_all.45.red_ref.sums1_ref, f32[128,128]{1,0:T(8,128)S(1)} %get-tuple-element.83.shift0_ref, f32[128,128]{1,0:T(8,128)S(1)} %get-tuple-element.84.shift1_ref, f32[128,128]{1,0:T(8,128)S(1)} %get-tuple-element.85.shift2_ref, ...), custom_call_target="tpu_custom_call" | custom-call | flops 1000000000 | bytes 720896 | tf_op jit(solution)/shard_map/square/pallas_call | solution.py:478
  166.3 4.3 %all-to-all-done.7 = f32[32,16,128]{2,1,0:T(8,128)S(1)} async-done(((f32[32,16,128]{2,1,0:T(8,128)}), f32[32,16,128]{2,1,0:T(8,128)S(1)}, u32[]{:S(2)}, u32[]{:S(2)}) %all-to-all-start.7) | async-done | bytes 262176 | tf_op jit(solution)/shard_map/all_to_all | solution.py:49
  171.3 11.6 %final.1 = (f32[1280,128]{1,0:T(8,128)}, f32[1280,128]{1,0:T(8,128)}) custom-call(f32[512,128]{1,0:T(8,128)} %bitcast.17, f32[1280,256]{1,0:T(8,128)} %copy-done.6, f32[1280,256]{1,0:T(8,128)} %copy-done, f32[1280,256]{1,0:T(8,128)} %copy-done.1, f32[1280,256]{1,0:T(8,128)} %copy-done.3, f32[8,128,128]{2,1,0:T(8,128)} %copy-done.7), custom_call_target="tpu_custom_call" | custom-call | bytes 6029312 | tf_op jit(solution)/shard_map/final/pallas_call | solution.py:478
  (61 shorter events, 18.9 us)
Async XLA Ops:
  0.6 25.9 %copy-start.4 = (bf16[480,320]{1,0:T(8,128)(2,1)S(1)}, bf16[480,320]{1,0:T(8,128)(2,1)}, u32[]{:S(2)}) copy-start(bf16[480,320]{1,0:T(8,128)(2,1)} %constant.2.clone.picks_ref.refs_1_.refs_2_) | copy-start | bytes 921604
  2.5 39.0 %copy-start.14 = (f32[4,320]{1,0:T(4,128)S(1)}, f32[4,320]{1,0:T(4,128)}, u32[]{:S(2)}) copy-start(f32[4,320]{1,0:T(4,128)} %damping_ref.7) | copy-start | bytes 15364
  35.2 101.5 %copy-start = (f32[1280,256]{1,0:T(8,128)}, f32[1280,256]{1,0:T(8,128)S(1)}, u32[]{:S(2)}) copy-start(f32[1280,256]{1,0:T(8,128)S(1)} %get-tuple-element.51.field_ref.refs_0_.v0_ref) | copy-start | bytes 3932164
  35.2 10.1 %collective-permute-start = (bf16[4,80,256]{2,1,0:T(8,128)(2,1)S(1)}, bf16[4,80,256]{2,1,0:T(8,128)(2,1)S(1)}, u32[]{:S(2)}, u32[]{:S(2)}) collective-permute-start(bf16[4,80,256]{2,1,0:T(8,128)(2,1)S(1)} %get-tuple-element.46), channel_id=1, source_target_pairs={{0,4},{4,8},{8,12},{12,16},{16,20},{20,24},{24,28},{1,5},{5,9},{9,... | collective-permute-start | bytes 491528 | tf_op jit(solution)/shard_map/ppermute | solution.py:26
  37.7 7.7 %collective-permute-start.1 = (bf16[4,80,256]{2,1,0:T(8,128)(2,1)S(1)}, bf16[4,80,256]{2,1,0:T(8,128)(2,1)S(1)}, u32[]{:S(2)}, u32[]{:S(2)}) collective-permute-start(bf16[4,80,256]{2,1,0:T(8,128)(2,1)S(1)} %get-tuple-element.47), channel_id=1, source_target_pairs={{4,0},{8,4},{12,8},{16,12},{20,16},{24,20},{28,24},{5,1},{9,5},{13... | collective-permute-start | bytes 491528 | tf_op jit(solution)/shard_map/ppermute | solution.py:26
  39.7 5.6 %collective-permute-start.2 = (bf16[2,80,256]{2,1,0:T(8,128)(2,1)S(1)}, bf16[2,80,256]{2,1,0:T(8,128)(2,1)S(1)}, u32[]{:S(2)}, u32[]{:S(2)}) collective-permute-start(bf16[2,80,256]{2,1,0:T(8,128)(2,1)S(1)} %get-tuple-element.48), channel_id=1, source_target_pairs={{3,0},{0,1},{1,2},{2,3},{7,4},{4,5},{5,6},{6,7},{11,8},{8,9},{9,10... | collective-permute-start | bytes 245768 | tf_op jit(solution)/shard_map/ppermute | solution.py:32
  39.8 5.5 %collective-permute-start.3 = (bf16[2,80,256]{2,1,0:T(8,128)(2,1)S(1)}, bf16[2,80,256]{2,1,0:T(8,128)(2,1)S(1)}, u32[]{:S(2)}, u32[]{:S(2)}) collective-permute-start(bf16[2,80,256]{2,1,0:T(8,128)(2,1)S(1)} %get-tuple-element.49), channel_id=1, source_target_pairs={{1,0},{2,1},{3,2},{0,3},{5,4},{6,5},{7,6},{4,7},{9,8},{10,9},{11,1... | collective-permute-start | bytes 245768 | tf_op jit(solution)/shard_map/ppermute | solution.py:32
  41.5 1.2 copy-start.15
  42.7 2.8 %copy-start.2 = (bf16[4,320,480]{2,1,0:T(8,128)(2,1)S(1)}, bf16[4,320,480]{2,1,0:T(8,128)(2,1)}, u32[]{:S(2)}) copy-start(bf16[4,320,480]{2,1,0:T(8,128)(2,1)} %face_ref.5) | copy-start | bytes 3686404
  42.7 2.8 %copy-start.8 = (s32[4,6]{1,0:T(4,128)S(1)}, s32[4,6]{1,0:T(4,128)}, u32[]{:S(2)}) copy-start(s32[4,6]{1,0:T(4,128)} %list_ref.5) | copy-start | bytes 292
  70.9 13.9 %copy-start.16 = (bf16[4,320,320]{2,1,0:T(8,128)(2,1)S(1)}, bf16[4,320,320]{2,1,0:T(8,128)(2,1)}, u32[]{:S(2)}) copy-start(bf16[4,320,320]{2,1,0:T(8,128)(2,1)} %diag_ref.5) | copy-start | bytes 2457604
  79.0 57.7 %copy-start.1 = (f32[1280,256]{1,0:T(8,128)}, f32[1280,256]{1,0:T(8,128)S(1)}, u32[]{:S(2)}) copy-start(f32[1280,256]{1,0:T(8,128)S(1)} %get-tuple-element.62.field_ref.refs_1_.v1_ref) | copy-start | bytes 3932164
  79.0 8.6 %collective-permute-start.4 = (bf16[4,80,256]{2,1,0:T(8,128)(2,1)S(1)}, bf16[4,80,256]{2,1,0:T(8,128)(2,1)S(1)}, u32[]{:S(2)}, u32[]{:S(2)}) collective-permute-start(bf16[4,80,256]{2,1,0:T(8,128)(2,1)S(1)} %get-tuple-element.58), channel_id=1, source_target_pairs={{0,4},{4,8},{8,12},{12,16},{16,20},{20,24},{24,28},{1,5},{5,9},{9,... | collective-permute-start | bytes 491528 | tf_op jit(solution)/shard_map/ppermute | solution.py:26
  81.6 7.6 %collective-permute-start.5 = (bf16[4,80,256]{2,1,0:T(8,128)(2,1)S(1)}, bf16[4,80,256]{2,1,0:T(8,128)(2,1)S(1)}, u32[]{:S(2)}, u32[]{:S(2)}) collective-permute-start(bf16[4,80,256]{2,1,0:T(8,128)(2,1)S(1)} %get-tuple-element.59), channel_id=1, source_target_pairs={{4,0},{8,4},{12,8},{16,12},{20,16},{24,20},{28,24},{5,1},{9,5},{13... | collective-permute-start | bytes 491528 | tf_op jit(solution)/shard_map/ppermute | solution.py:26
  82.9 4.6 %collective-permute-start.6 = (bf16[2,80,256]{2,1,0:T(8,128)(2,1)S(1)}, bf16[2,80,256]{2,1,0:T(8,128)(2,1)S(1)}, u32[]{:S(2)}, u32[]{:S(2)}) collective-permute-start(bf16[2,80,256]{2,1,0:T(8,128)(2,1)S(1)} %get-tuple-element.60), channel_id=1, source_target_pairs={{3,0},{0,1},{1,2},{2,3},{7,4},{4,5},{5,6},{6,7},{11,8},{8,9},{9,10... | collective-permute-start | bytes 245768 | tf_op jit(solution)/shard_map/ppermute | solution.py:32
  83.0 4.6 %collective-permute-start.7 = (bf16[2,80,256]{2,1,0:T(8,128)(2,1)S(1)}, bf16[2,80,256]{2,1,0:T(8,128)(2,1)S(1)}, u32[]{:S(2)}, u32[]{:S(2)}) collective-permute-start(bf16[2,80,256]{2,1,0:T(8,128)(2,1)S(1)} %get-tuple-element.61), channel_id=1, source_target_pairs={{1,0},{2,1},{3,2},{0,3},{5,4},{6,5},{7,6},{4,7},{9,8},{10,9},{11,1... | collective-permute-start | bytes 245768 | tf_op jit(solution)/shard_map/ppermute | solution.py:32
  89.2 28.1 %copy-start.10 = (s32[1,2,4]{2,1,0:T(2,128)S(1)}, s32[1,2,4]{2,1,0:T(2,128)}, u32[]{:S(2)}) copy-start(s32[1,2,4]{2,1,0:T(2,128)} %refs_3_.3) | copy-start | bytes 100
  89.2 28.1 %copy-start.12 = (s32[1,2,2]{2,1,0:T(2,128)S(1)}, s32[1,2,2]{2,1,0:T(2,128)}, u32[]{:S(2)}) copy-start(s32[1,2,2]{2,1,0:T(2,128)} %refs_4_.1) | copy-start | bytes 52
  126.5 10.2 %copy-start.3 = (f32[1280,256]{1,0:T(8,128)}, f32[1280,256]{1,0:T(8,128)S(1)}, u32[]{:S(2)}) copy-start(f32[1280,256]{1,0:T(8,128)S(1)} %get-tuple-element.75.field_ref.refs_2_.v2_ref) | copy-start | bytes 3932164
  126.5 8.9 %collective-permute-start.8 = (bf16[4,80,256]{2,1,0:T(8,128)(2,1)S(1)}, bf16[4,80,256]{2,1,0:T(8,128)(2,1)S(1)}, u32[]{:S(2)}, u32[]{:S(2)}) collective-permute-start(bf16[4,80,256]{2,1,0:T(8,128)(2,1)S(1)} %get-tuple-element.71), channel_id=1, source_target_pairs={{0,4},{4,8},{8,12},{12,16},{16,20},{20,24},{24,28},{1,5},{5,9},{9,... | collective-permute-start | bytes 491528 | tf_op jit(solution)/shard_map/ppermute | solution.py:26
  129.3 7.4 %collective-permute-start.9 = (bf16[4,80,256]{2,1,0:T(8,128)(2,1)S(1)}, bf16[4,80,256]{2,1,0:T(8,128)(2,1)S(1)}, u32[]{:S(2)}, u32[]{:S(2)}) collective-permute-start(bf16[4,80,256]{2,1,0:T(8,128)(2,1)S(1)} %get-tuple-element.72), channel_id=1, source_target_pairs={{4,0},{8,4},{12,8},{16,12},{20,16},{24,20},{28,24},{5,1},{9,5},{13... | collective-permute-start | bytes 491528 | tf_op jit(solution)/shard_map/ppermute | solution.py:26
  130.6 4.8 %collective-permute-start.10 = (bf16[2,80,256]{2,1,0:T(8,128)(2,1)S(1)}, bf16[2,80,256]{2,1,0:T(8,128)(2,1)S(1)}, u32[]{:S(2)}, u32[]{:S(2)}) collective-permute-start(bf16[2,80,256]{2,1,0:T(8,128)(2,1)S(1)} %get-tuple-element.73), channel_id=1, source_target_pairs={{3,0},{0,1},{1,2},{2,3},{7,4},{4,5},{5,6},{6,7},{11,8},{8,9},{9,10... | collective-permute-start | bytes 245768 | tf_op jit(solution)/shard_map/ppermute | solution.py:32
  130.6 4.7 %collective-permute-start.11 = (bf16[2,80,256]{2,1,0:T(8,128)(2,1)S(1)}, bf16[2,80,256]{2,1,0:T(8,128)(2,1)S(1)}, u32[]{:S(2)}, u32[]{:S(2)}) collective-permute-start(bf16[2,80,256]{2,1,0:T(8,128)(2,1)S(1)} %get-tuple-element.74), channel_id=1, source_target_pairs={{1,0},{2,1},{3,2},{0,3},{5,4},{6,5},{7,6},{4,7},{9,8},{10,9},{11,1... | collective-permute-start | bytes 245768 | tf_op jit(solution)/shard_map/ppermute | solution.py:32
  157.4 13.2 %all-to-all-start.7 = ((f32[32,16,128]{2,1,0:T(8,128)}), f32[32,16,128]{2,1,0:T(8,128)S(1)}, u32[]{:S(2)}, u32[]{:S(2)}) async-start(f32[32,16,128]{2,1,0:T(8,128)} %add_up.7), calls=%async_computation.7 | async-start | bytes 524288 | tf_op jit(solution)/shard_map/all_to_all | solution.py:49
  (7 other events, 5.8 us)

commit v3 on v2

--- a/solution.py
+++ b/solution.py
@@ -413,12 +413,12 @@
     goal = mm(reach, right)
     _, iq = factor(gram + mm_nt(reach, reach))
     y2 = mm_tn(iq, mm(iq, goal))
-    z = mm(reach_in, right - mm_tn(reach, y2))
+    z = mm_pieces([reach_in], pieces_of(right - mm_tn(reach, y2)))
     z = [z[k * width : (k + 1) * width] for k in range(3)]
     hy = mm_tn(jnp.concatenate([coeffs, shift2], 1), y2)
     hy = [hy[k * width : (k + 1) * width] for k in range(4)]
     y1 = -mm_tn(i2, z[2] + hy[2] + hy[3])
-    y0 = -mm_tn(i1, z[1] + hy[1]) - mm(mixed, y1)
+    y0 = -mm_tn(i1, z[1] + hy[1]) - mm_pieces([mixed], pieces_of(y1))
     left = grid_of((width, width), 1) < half
     rows = []
     for y, w in ((y0, z[0] + hy[0]), (y1, z[1] + hy[1]), (y2, z[2] + hy[2]), (0.0 * y2, -y2)):
@@ -441,8 +441,11 @@
     def _(e):
         at = rows_of(e, size)
 
-        cuts = [slice(h * width, (h + 1) * width) for h in range(2)]
-        first, second = [mm_pieces([fields[j, at, cut] for j in range(4)], weights) for cut in cuts]
+        parts = [
+            jnp.concatenate([fields[j, at, :width], fields[j, at, width:]], 0) for j in range(4)
+        ]
+        out = mm_pieces(parts, weights)
+        first, second = out[:size], out[size:]
         solved[at, :] = jnp.where(lanes, first, pltpu.roll(second, half, 1))
         left_over[at, :] = jnp.where(lanes, pltpu.roll(first, half, 1), second)
         for copy in copies(e):

time: 184 us -> 183 us (level)
  no operation moved by 1% of the time
where the time goes in v3:
time: 183 us
  blocking collectives  84.3 us (46%)
  Pallas kernels  62.2 us (34%)
  starting transfers between devices  19.9 us (11%)
  waiting for transfers between devices  7.45 us (4%)
  local copies, waits for them, and re-layouts  6.97 us (4%)
    pallas_call x16, Pallas kernels, call(): pl.pallas_call(kernel, name=name, out_shape=[jax.ShapeDtypeStruct(shape,...  62.2 us
    all_to_all x4, blocking collectives, exchange(): parts = lax.all_to_all(shares, AXES, 0, 0)  53.9 us
    all_to_all x3, blocking collectives, exchange(): return lax.all_to_all(mine, AXES, 0, 0)  30.4 us
    ppermute x6, starting transfers between devices, passed_along(): lax.ppermute(value, axis, [(source, source + steps) for source in range(f...  11.8 us
    unnamed x36, local copies, waits for them, and re-layouts  6.97 us
    ppermute x6, starting transfers between devices, shifted(): return lax.ppermute(block, axis, route)  5.37 us
    all_to_all x1, waiting for transfers between devices, exchange(): return lax.all_to_all(mine, AXES, 0, 0)  4.27 us
  transfers between devices with their start and end apart: 13, of which 4 were waited for; matrix products, arithmetic and copies ran while one was open for 0% of the time, Pallas kernels for 7%

profile of v3, /device:TPU:0, one launch (start us, length us, event | category | flops | bytes accessed | tf_op | source)
XLA Modules:
  0.0 182.6 jit_solution(12830889951043606885)
XLA Ops:
  2.9 14.5 %all_to_all.40.parts_ref = f32[32,4,128]{2,1,0:T(4,128)S(1)} all-to-all(f32[32,4,128]{2,1,0:T(4,128)S(1)} %bitcast.15), channel_id=1, replica_groups=mesh['stream'=8,'cross'=4] {'stream','cross'}, dimensions={0} | all-to-all | bytes 131072 | tf_op jit(solution)/shard_map/all_to_all | solution.py:47
  17.4 9.1 %all_to_all.41 = f32[32,4,128]{2,1,0:T(4,128)S(1)} all-to-all(f32[32,4,128]{2,1,0:T(4,128)S(1)} %add_up.4), channel_id=1, replica_groups=mesh['stream'=8,'cross'=4] {'stream','cross'}, dimensions={0} | all-to-all | bytes 131072 | tf_op jit(solution)/shard_map/all_to_all | solution.py:49
  27.9 7.3 %start.1 = (f32[1280,256]{1,0:T(8,128)S(1)}, bf16[24,80,256]{2,1,0:T(8,128)(2,1)S(1)}, bf16[4,80,256]{2,1,0:T(8,128)(2,1)S(1)}, bf16[4,80,256]{2,1,0:T(8,128)(2,...) custom-call(f32[128,128]{1,0:T(8,128)S(1)} %bitcast.13, ...), custom_call_target="tpu_custom_call" | custom-call | bytes 1028144 | tf_op jit(solution)/shard_map/start/pallas_call | solution.py:481
  35.2 2.5 %collective-permute-start = (bf16[4,80,256]{2,1,0:T(8,128)(2,1)S(1)}, bf16[4,80,256]{2,1,0:T(8,128)(2,1)S(1)}, u32[]{:S(2)}, u32[]{:S(2)}) collective-permute-start(bf16[4,80,256]{2,1,0:T(8,128)(2,1)S(1)} %get-tuple-element.46), channel_id=1, source_target_pairs={{0,4},{4,8},{8,12},{12,16},{16,20},{20,24},{24,28},{1,5},{5,9},{9,... | collective-permute-start | bytes 491528 | tf_op jit(solution)/shard_map/ppermute | solution.py:26
  42.7 2.5 %inner.3 = (f32[1280,256]{1,0:T(8,128)S(1)}, f32[128,128]{1,0:T(8,128)S(1)}, f32[128,128]{1,0:T(8,128)S(1)}, f32[128,128]{1,0:T(8,128)S(1)}) custom-call(f32[1]{0:T(128)S(6)} %copy.11.omega_ref, f32[8,128]{1,0:T(8,128)S(1)} %get-tuple-element.50.center_ref, f32[4,320]{1,0:T(4,128)S(1)} %copy-done.14, bf16[4,320,320]{2,1,0:T(8,128)(2,1)S(1)} %copy-done.15, ...), custom_call_target="tpu_custom_call" | custom-call | flops 1000000000 | bytes 2270212 | tf_op jit(solution)/shard_map/inner/pallas_call | solution.py:481
  45.5 3.4 %outer.3 = (f32[1280,256]{1,0:T(8,128)S(1)}, f32[256,128]{1,0:T(8,128)S(1)}) custom-call(s32[4,6]{1,0:T(4,128)S(1)} %copy-done.8, bf16[24,80,256]{2,1,0:T(8,128)(2,1)S(1)} %get-tuple-element.45.traces_ref, bf16[4,80,256]{2,1,0:T(8,128)(2,1)S(1)} %collective-permute-done.prev_ref, bf16[4,80,256]{2,1,0:T(8,128)(2,1)S(1)} %collective-permute-done.1.next_ref, ...), custom_call_target="tpu_custom_call" | custom-call | bytes 5324896 | tf_op jit(solution)/shard_map/outer/pallas_call | solution.py:481
  48.9 11.9 %all_to_all.42.parts_ref = f32[32,8,128]{2,1,0:T(8,128)S(1)} all-to-all(f32[32,8,128]{2,1,0:T(8,128)S(1)} %bitcast.16), channel_id=1, replica_groups=mesh['stream'=8,'cross'=4] {'stream','cross'}, dimensions={0} | all-to-all | bytes 262144 | tf_op jit(solution)/shard_map/all_to_all | solution.py:47
  60.9 10.0 %all_to_all.43 = f32[32,8,128]{2,1,0:T(8,128)S(1)} all-to-all(f32[32,8,128]{2,1,0:T(8,128)S(1)} %add_up.5), channel_id=1, replica_groups=mesh['stream'=8,'cross'=4] {'stream','cross'}, dimensions={0} | all-to-all | bytes 262144 | tf_op jit(solution)/shard_map/all_to_all | solution.py:49
  70.9 8.1 %next.2 = (f32[1280,256]{1,0:T(8,128)S(1)}, bf16[24,80,256]{2,1,0:T(8,128)(2,1)S(1)}, bf16[4,80,256]{2,1,0:T(8,128)(2,1)S(1)}, bf16[4,80,256]{2,1,0:T(8,128)(2,1...) custom-call(f32[256,128]{1,0:T(8,128)S(1)} %bitcast.11, ...), custom_call_target="tpu_custom_call" | custom-call | bytes 3059760 | tf_op jit(solution)/shard_map/next/pallas_call | solution.py:481
  79.0 2.6 %collective-permute-start.4 = (bf16[4,80,256]{2,1,0:T(8,128)(2,1)S(1)}, bf16[4,80,256]{2,1,0:T(8,128)(2,1)S(1)}, u32[]{:S(2)}, u32[]{:S(2)}) collective-permute-start(bf16[4,80,256]{2,1,0:T(8,128)(2,1)S(1)} %get-tuple-element.58), channel_id=1, source_target_pairs={{0,4},{4,8},{8,12},{12,16},{16,20},{20,24},{24,28},{1,5},{5,9},{9,... | collective-permute-start | bytes 491528 | tf_op jit(solution)/shard_map/ppermute | solution.py:26
  83.0 1.7 collective-permute-start.7
  84.7 2.8 %inner.4 = (f32[1280,256]{1,0:T(8,128)S(1)}, f32[128,128]{1,0:T(8,128)S(1)}, f32[128,128]{1,0:T(8,128)S(1)}, f32[128,128]{1,0:T(8,128)S(1)}) custom-call(f32[1]{0:T(128)S(6)} %copy.11.omega_ref, f32[8,128]{1,0:T(8,128)S(1)} %get-tuple-element.50.center_ref, f32[4,320]{1,0:T(4,128)S(1)} %copy-done.14, bf16[4,320,320]{2,1,0:T(8,128)(2,1)S(1)} %copy-done.16, ...), custom_call_target="tpu_custom_call" | custom-call | flops 1000000000 | bytes 2401284 | tf_op jit(solution)/shard_map/inner/pallas_call | solution.py:481
  89.3 4.1 %outer.4 = (f32[1280,256]{1,0:T(8,128)S(1)}, f32[32,4,384]{2,1,0:T(4,128)S(1)}) custom-call(s32[4,6]{1,0:T(4,128)S(1)} %copy-done.8, bf16[24,80,256]{2,1,0:T(8,128)(2,1)S(1)} %get-tuple-element.57.traces_ref, bf16[4,80,256]{2,1,0:T(8,128)(2,1)S(1)} %collective-permute-done.4.prev_ref, bf16[4,80,256]{2,1,0:T(8,128)(2,1)S(1)} %collective-permute-done.5.next_ref, ...), custom_call_target="tpu_custom_call" | custom-call | bytes 6635616 | tf_op jit(solution)/shard_map/outer/pallas_call | solution.py:481
  93.3 12.6 %all_to_all.44.parts_ref = f32[32,4,384]{2,1,0:T(4,128)S(1)} all-to-all(f32[32,4,384]{2,1,0:T(4,128)S(1)} %get-tuple-element.68), channel_id=1, replica_groups=mesh['stream'=8,'cross'=4] {'stream','cross'}, dimensions={0} | all-to-all | bytes 393216 | tf_op jit(solution)/shard_map/all_to_all | solution.py:47
  106.0 11.4 %all_to_all.45.red_ref.sums1_ref = f32[32,4,384]{2,1,0:T(4,128)S(1)} all-to-all(f32[32,4,384]{2,1,0:T(4,128)S(1)} %add_up.6), channel_id=1, replica_groups=mesh['stream'=8,'cross'=4] {'stream','cross'}, dimensions={0} | all-to-all | bytes 393216 | tf_op jit(solution)/shard_map/all_to_all | solution.py:49
  117.3 9.1 %next.3 = (f32[1280,256]{1,0:T(8,128)S(1)}, bf16[24,80,256]{2,1,0:T(8,128)(2,1)S(1)}, bf16[4,80,256]{2,1,0:T(8,128)(2,1)S(1)}, bf16[4,80,256]{2,1,0:T(8,128)(2,1...) custom-call(f32[32,4,384]{2,1,0:T(4,128)S(1)} %all_to_all.45.red_ref, ...), custom_call_target="tpu_custom_call" | custom-call | bytes 4436016 | tf_op jit(solution)/shard_map/next/pallas_call | solution.py:481
  126.5 2.8 %collective-permute-start.8 = (bf16[4,80,256]{2,1,0:T(8,128)(2,1)S(1)}, bf16[4,80,256]{2,1,0:T(8,128)(2,1)S(1)}, u32[]{:S(2)}, u32[]{:S(2)}) collective-permute-start(bf16[4,80,256]{2,1,0:T(8,128)(2,1)S(1)} %get-tuple-element.71), channel_id=1, source_target_pairs={{0,4},{4,8},{8,12},{12,16},{16,20},{20,24},{24,28},{1,5},{5,9},{9,... | collective-permute-start | bytes 491528 | tf_op jit(solution)/shard_map/ppermute | solution.py:26
  132.4 3.0 %inner.5 = (f32[1280,256]{1,0:T(8,128)S(1)}, f32[128,128]{1,0:T(8,128)S(1)}, f32[128,128]{1,0:T(8,128)}, f32[128,128]{1,0:T(8,128)}) custom-call(f32[1]{0:T(128)S(6)} %copy.11.omega_ref, f32[8,128]{1,0:T(8,128)S(1)} %get-tuple-element.50.center_ref, f32[4,320]{1,0:T(4,128)S(1)} %copy-done.14, bf16[4,320,320]{2,1,0:T(8,128)(2,1)S(1)} %copy-done.16, ...), custom_call_target="tpu_custom_call" | custom-call | flops 1000000000 | bytes 2401284 | tf_op jit(solution)/shard_map/inner/pallas_call | solution.py:481
  136.7 4.1 %outer.5 = (f32[1280,256]{1,0:T(8,128)S(1)}, f32[512,128]{1,0:T(8,128)S(1)}) custom-call(s32[4,6]{1,0:T(4,128)S(1)} %copy-done.8, bf16[24,80,256]{2,1,0:T(8,128)(2,1)S(1)} %get-tuple-element.70.traces_ref, bf16[4,80,256]{2,1,0:T(8,128)(2,1)S(1)} %collective-permute-done.8.prev_ref, bf16[4,80,256]{2,1,0:T(8,128)(2,1)S(1)} %collective-permute-done.9.next_ref, ...), custom_call_target="tpu_custom_call" | custom-call | bytes 7946336 | tf_op jit(solution)/shard_map/outer/pallas_call | solution.py:481
  141.8 14.8 %all_to_all.46.parts_ref = f32[32,16,128]{2,1,0:T(8,128)S(1)} all-to-all(f32[32,16,128]{2,1,0:T(8,128)S(1)} %bitcast.14), channel_id=1, replica_groups=mesh['stream'=8,'cross'=4] {'stream','cross'}, dimensions={0} | all-to-all | bytes 524288 | tf_op jit(solution)/shard_map/all_to_all | solution.py:47
  157.4 2.8 %all-to-all-start.7 = ((f32[32,16,128]{2,1,0:T(8,128)}), f32[32,16,128]{2,1,0:T(8,128)S(1)}, u32[]{:S(2)}, u32[]{:S(2)}) async-start(f32[32,16,128]{2,1,0:T(8,128)} %add_up.7), calls=%async_computation.7 | async-start | bytes 524288 | tf_op jit(solution)/shard_map/all_to_all | solution.py:49
  160.3 5.3 %square.1.pack_ref = f32[8,128,128]{2,1,0:T(8,128)S(1)} custom-call(f32[256,128]{1,0:T(8,128)S(1)} %bitcast.12, f32[32,4,384]{2,1,0:T(4,128)S(1)} %all_to_all.45.red_ref.sums1_ref, f32[128,128]{1,0:T(8,128)S(1)} %get-tuple-element.83.shift0_ref, f32[128,128]{1,0:T(8,128)S(1)} %get-tuple-element.84.shift1_ref, f32[128,128]{1,0:T(8,128)S(1)} %get-tuple-element.85.shift2_ref, ...), custom_call_target="tpu_custom_call" | custom-call | flops 1000000000 | bytes 720896 | tf_op jit(solution)/shard_map/square/pallas_call | solution.py:481
  166.3 4.3 %all-to-all-done.7 = f32[32,16,128]{2,1,0:T(8,128)S(1)} async-done(((f32[32,16,128]{2,1,0:T(8,128)}), f32[32,16,128]{2,1,0:T(8,128)S(1)}, u32[]{:S(2)}, u32[]{:S(2)}) %all-to-all-start.7) | async-done | bytes 262176 | tf_op jit(solution)/shard_map/all_to_all | solution.py:49
  171.3 11.1 %final.1 = (f32[1280,128]{1,0:T(8,128)}, f32[1280,128]{1,0:T(8,128)}) custom-call(f32[512,128]{1,0:T(8,128)} %bitcast.17, f32[1280,256]{1,0:T(8,128)} %copy-done.6, f32[1280,256]{1,0:T(8,128)} %copy-done, f32[1280,256]{1,0:T(8,128)} %copy-done.1, f32[1280,256]{1,0:T(8,128)} %copy-done.3, f32[8,128,128]{2,1,0:T(8,128)} %copy-done.7), custom_call_target="tpu_custom_call" | custom-call | bytes 6029312 | tf_op jit(solution)/shard_map/final/pallas_call | solution.py:481
  (61 shorter events, 18.9 us)
Async XLA Ops:
  0.6 25.9 %copy-start.4 = (bf16[480,320]{1,0:T(8,128)(2,1)S(1)}, bf16[480,320]{1,0:T(8,128)(2,1)}, u32[]{:S(2)}) copy-start(bf16[480,320]{1,0:T(8,128)(2,1)} %constant.2.clone.picks_ref.refs_1_.refs_2_) | copy-start | bytes 921604
  2.5 39.0 %copy-start.14 = (f32[4,320]{1,0:T(4,128)S(1)}, f32[4,320]{1,0:T(4,128)}, u32[]{:S(2)}) copy-start(f32[4,320]{1,0:T(4,128)} %damping_ref.7) | copy-start | bytes 15364
  35.2 101.5 %copy-start = (f32[1280,256]{1,0:T(8,128)}, f32[1280,256]{1,0:T(8,128)S(1)}, u32[]{:S(2)}) copy-start(f32[1280,256]{1,0:T(8,128)S(1)} %get-tuple-element.51.field_ref.refs_0_.v0_ref) | copy-start | bytes 3932164
  35.2 10.1 %collective-permute-start = (bf16[4,80,256]{2,1,0:T(8,128)(2,1)S(1)}, bf16[4,80,256]{2,1,0:T(8,128)(2,1)S(1)}, u32[]{:S(2)}, u32[]{:S(2)}) collective-permute-start(bf16[4,80,256]{2,1,0:T(8,128)(2,1)S(1)} %get-tuple-element.46), channel_id=1, source_target_pairs={{0,4},{4,8},{8,12},{12,16},{16,20},{20,24},{24,28},{1,5},{5,9},{9,... | collective-permute-start | bytes 491528 | tf_op jit(solution)/shard_map/ppermute | solution.py:26
  37.7 7.7 %collective-permute-start.1 = (bf16[4,80,256]{2,1,0:T(8,128)(2,1)S(1)}, bf16[4,80,256]{2,1,0:T(8,128)(2,1)S(1)}, u32[]{:S(2)}, u32[]{:S(2)}) collective-permute-start(bf16[4,80,256]{2,1,0:T(8,128)(2,1)S(1)} %get-tuple-element.47), channel_id=1, source_target_pairs={{4,0},{8,4},{12,8},{16,12},{20,16},{24,20},{28,24},{5,1},{9,5},{13... | collective-permute-start | bytes 491528 | tf_op jit(solution)/shard_map/ppermute | solution.py:26
  39.7 5.6 %collective-permute-start.2 = (bf16[2,80,256]{2,1,0:T(8,128)(2,1)S(1)}, bf16[2,80,256]{2,1,0:T(8,128)(2,1)S(1)}, u32[]{:S(2)}, u32[]{:S(2)}) collective-permute-start(bf16[2,80,256]{2,1,0:T(8,128)(2,1)S(1)} %get-tuple-element.48), channel_id=1, source_target_pairs={{3,0},{0,1},{1,2},{2,3},{7,4},{4,5},{5,6},{6,7},{11,8},{8,9},{9,10... | collective-permute-start | bytes 245768 | tf_op jit(solution)/shard_map/ppermute | solution.py:32
  39.8 5.5 %collective-permute-start.3 = (bf16[2,80,256]{2,1,0:T(8,128)(2,1)S(1)}, bf16[2,80,256]{2,1,0:T(8,128)(2,1)S(1)}, u32[]{:S(2)}, u32[]{:S(2)}) collective-permute-start(bf16[2,80,256]{2,1,0:T(8,128)(2,1)S(1)} %get-tuple-element.49), channel_id=1, source_target_pairs={{1,0},{2,1},{3,2},{0,3},{5,4},{6,5},{7,6},{4,7},{9,8},{10,9},{11,1... | collective-permute-start | bytes 245768 | tf_op jit(solution)/shard_map/ppermute | solution.py:32
  41.5 1.2 copy-start.15
  42.7 2.8 %copy-start.2 = (bf16[4,320,480]{2,1,0:T(8,128)(2,1)S(1)}, bf16[4,320,480]{2,1,0:T(8,128)(2,1)}, u32[]{:S(2)}) copy-start(bf16[4,320,480]{2,1,0:T(8,128)(2,1)} %face_ref.5) | copy-start | bytes 3686404
  42.7 2.8 %copy-start.8 = (s32[4,6]{1,0:T(4,128)S(1)}, s32[4,6]{1,0:T(4,128)}, u32[]{:S(2)}) copy-start(s32[4,6]{1,0:T(4,128)} %list_ref.5) | copy-start | bytes 292
  70.9 13.9 %copy-start.16 = (bf16[4,320,320]{2,1,0:T(8,128)(2,1)S(1)}, bf16[4,320,320]{2,1,0:T(8,128)(2,1)}, u32[]{:S(2)}) copy-start(bf16[4,320,320]{2,1,0:T(8,128)(2,1)} %diag_ref.5) | copy-start | bytes 2457604
  79.0 57.7 %copy-start.1 = (f32[1280,256]{1,0:T(8,128)}, f32[1280,256]{1,0:T(8,128)S(1)}, u32[]{:S(2)}) copy-start(f32[1280,256]{1,0:T(8,128)S(1)} %get-tuple-element.62.field_ref.refs_1_.v1_ref) | copy-start | bytes 3932164
  79.0 8.6 %collective-permute-start.4 = (bf16[4,80,256]{2,1,0:T(8,128)(2,1)S(1)}, bf16[4,80,256]{2,1,0:T(8,128)(2,1)S(1)}, u32[]{:S(2)}, u32[]{:S(2)}) collective-permute-start(bf16[4,80,256]{2,1,0:T(8,128)(2,1)S(1)} %get-tuple-element.58), channel_id=1, source_target_pairs={{0,4},{4,8},{8,12},{12,16},{16,20},{20,24},{24,28},{1,5},{5,9},{9,... | collective-permute-start | bytes 491528 | tf_op jit(solution)/shard_map/ppermute | solution.py:26
  81.6 7.6 %collective-permute-start.5 = (bf16[4,80,256]{2,1,0:T(8,128)(2,1)S(1)}, bf16[4,80,256]{2,1,0:T(8,128)(2,1)S(1)}, u32[]{:S(2)}, u32[]{:S(2)}) collective-permute-start(bf16[4,80,256]{2,1,0:T(8,128)(2,1)S(1)} %get-tuple-element.59), channel_id=1, source_target_pairs={{4,0},{8,4},{12,8},{16,12},{20,16},{24,20},{28,24},{5,1},{9,5},{13... | collective-permute-start | bytes 491528 | tf_op jit(solution)/shard_map/ppermute | solution.py:26
  82.9 4.6 %collective-permute-start.6 = (bf16[2,80,256]{2,1,0:T(8,128)(2,1)S(1)}, bf16[2,80,256]{2,1,0:T(8,128)(2,1)S(1)}, u32[]{:S(2)}, u32[]{:S(2)}) collective-permute-start(bf16[2,80,256]{2,1,0:T(8,128)(2,1)S(1)} %get-tuple-element.60), channel_id=1, source_target_pairs={{3,0},{0,1},{1,2},{2,3},{7,4},{4,5},{5,6},{6,7},{11,8},{8,9},{9,10... | collective-permute-start | bytes 245768 | tf_op jit(solution)/shard_map/ppermute | solution.py:32
  83.0 4.6 %collective-permute-start.7 = (bf16[2,80,256]{2,1,0:T(8,128)(2,1)S(1)}, bf16[2,80,256]{2,1,0:T(8,128)(2,1)S(1)}, u32[]{:S(2)}, u32[]{:S(2)}) collective-permute-start(bf16[2,80,256]{2,1,0:T(8,128)(2,1)S(1)} %get-tuple-element.61), channel_id=1, source_target_pairs={{1,0},{2,1},{3,2},{0,3},{5,4},{6,5},{7,6},{4,7},{9,8},{10,9},{11,1... | collective-permute-start | bytes 245768 | tf_op jit(solution)/shard_map/ppermute | solution.py:32
  89.3 28.1 %copy-start.10 = (s32[1,2,4]{2,1,0:T(2,128)S(1)}, s32[1,2,4]{2,1,0:T(2,128)}, u32[]{:S(2)}) copy-start(s32[1,2,4]{2,1,0:T(2,128)} %refs_3_.3) | copy-start | bytes 100
  89.3 28.1 %copy-start.12 = (s32[1,2,2]{2,1,0:T(2,128)S(1)}, s32[1,2,2]{2,1,0:T(2,128)}, u32[]{:S(2)}) copy-start(s32[1,2,2]{2,1,0:T(2,128)} %refs_4_.1) | copy-start | bytes 52
  126.5 10.2 %copy-start.3 = (f32[1280,256]{1,0:T(8,128)}, f32[1280,256]{1,0:T(8,128)S(1)}, u32[]{:S(2)}) copy-start(f32[1280,256]{1,0:T(8,128)S(1)} %get-tuple-element.75.field_ref.refs_2_.v2_ref) | copy-start | bytes 3932164
  126.5 8.9 %collective-permute-start.8 = (bf16[4,80,256]{2,1,0:T(8,128)(2,1)S(1)}, bf16[4,80,256]{2,1,0:T(8,128)(2,1)S(1)}, u32[]{:S(2)}, u32[]{:S(2)}) collective-permute-start(bf16[4,80,256]{2,1,0:T(8,128)(2,1)S(1)} %get-tuple-element.71), channel_id=1, source_target_pairs={{0,4},{4,8},{8,12},{12,16},{16,20},{20,24},{24,28},{1,5},{5,9},{9,... | collective-permute-start | bytes 491528 | tf_op jit(solution)/shard_map/ppermute | solution.py:26
  129.3 7.4 %collective-permute-start.9 = (bf16[4,80,256]{2,1,0:T(8,128)(2,1)S(1)}, bf16[4,80,256]{2,1,0:T(8,128)(2,1)S(1)}, u32[]{:S(2)}, u32[]{:S(2)}) collective-permute-start(bf16[4,80,256]{2,1,0:T(8,128)(2,1)S(1)} %get-tuple-element.72), channel_id=1, source_target_pairs={{4,0},{8,4},{12,8},{16,12},{20,16},{24,20},{28,24},{5,1},{9,5},{13... | collective-permute-start | bytes 491528 | tf_op jit(solution)/shard_map/ppermute | solution.py:26
  130.6 4.8 %collective-permute-start.10 = (bf16[2,80,256]{2,1,0:T(8,128)(2,1)S(1)}, bf16[2,80,256]{2,1,0:T(8,128)(2,1)S(1)}, u32[]{:S(2)}, u32[]{:S(2)}) collective-permute-start(bf16[2,80,256]{2,1,0:T(8,128)(2,1)S(1)} %get-tuple-element.73), channel_id=1, source_target_pairs={{3,0},{0,1},{1,2},{2,3},{7,4},{4,5},{5,6},{6,7},{11,8},{8,9},{9,10... | collective-permute-start | bytes 245768 | tf_op jit(solution)/shard_map/ppermute | solution.py:32
  130.6 4.7 %collective-permute-start.11 = (bf16[2,80,256]{2,1,0:T(8,128)(2,1)S(1)}, bf16[2,80,256]{2,1,0:T(8,128)(2,1)S(1)}, u32[]{:S(2)}, u32[]{:S(2)}) collective-permute-start(bf16[2,80,256]{2,1,0:T(8,128)(2,1)S(1)} %get-tuple-element.74), channel_id=1, source_target_pairs={{1,0},{2,1},{3,2},{0,3},{5,4},{6,5},{7,6},{4,7},{9,8},{10,9},{11,1... | collective-permute-start | bytes 245768 | tf_op jit(solution)/shard_map/ppermute | solution.py:32
  157.4 13.2 %all-to-all-start.7 = ((f32[32,16,128]{2,1,0:T(8,128)}), f32[32,16,128]{2,1,0:T(8,128)S(1)}, u32[]{:S(2)}, u32[]{:S(2)}) async-start(f32[32,16,128]{2,1,0:T(8,128)} %add_up.7), calls=%async_computation.7 | async-start | bytes 524288 | tf_op jit(solution)/shard_map/all_to_all | solution.py:49
  (7 other events, 5.8 us)
